TPU v7x, 128 devices: a whole 4x4x4 slice. The times are simulated.
128 devices in a mesh: row: 8 (over x_lo, z), col: 16 (over x_hi, y, core).
Axes of the slice: x: 4 (x_hi: 2, x_lo: 2; x = x_hi * 2 + x_lo), y: 4, z: 4, core: 2. Of those that a mesh axis runs over, the one named last changes fastest.
Arguments:
- level_set: float32 [384, 384, 384], P('col', 'row'), may hold values from -7 to 7
- image: float32 [384, 384, 384], P('col', 'row'), may hold values from -6 to 6
Outputs:
- updated_level: float32 [384, 384, 384], P('col', 'row')
All inputs are finite; a program needn't handle non-finite values.
Results may differ from a plain program's by a relative error of at most 0.00021.
Values sent between devices are 32-bit elements; how exact they have to be, the bound alone decides.
A program may use at most 128 MiB of HBM per device.

v0:
```python
import jax
import jax.numpy as jnp
from jax import lax
from jax.sharding import PartitionSpec as P

RADIUS = 6


sigma_cells = 8.0
dt_step = 0.5
nu_diff = 0.1
eps_fit = 0.05


def extended(value, sides, width):
    for axis, dim in sides:
        devices, length = (lax.axis_size(axis), value.shape[dim])
        up = [(i, (i + 1) % devices) for i in range(devices)]
        down = [(j, i) for i, j in up]
        last = lax.slice_in_dim(value, length - width, length, axis=dim)
        first = lax.slice_in_dim(value, 0, width, axis=dim)
        before = lax.ppermute(last, axis, up)
        after = lax.ppermute(first, axis, down)
        value = jnp.concatenate([before, value, after], axis=dim)
    return value


def tap_weight(offset):
    tap_offsets = lax.iota(jnp.int32, 2 * RADIUS + 1) - RADIUS
    tap_float = tap_offsets.astype(jnp.float32)
    total_weight = jnp.sum(jnp.exp(-tap_float * tap_float / (2.0 * sigma_cells * sigma_cells)))
    off_float = offset.astype(jnp.float32)
    inside = jnp.abs(offset) <= RADIUS
    weights = jnp.where(
        inside, jnp.exp(-off_float * off_float / (2.0 * sigma_cells * sigma_cells)), 0.0
    )
    return weights / total_weight


def gauss_table(length):
    indices = lax.iota(jnp.int32, length)
    distance = jnp.abs(indices[:, None] - indices[None, :])
    distance = jnp.minimum(distance, length - distance)
    return tap_weight(distance)


def lines_along_x(fields, kernel_table):
    along_x = jnp.einsum("fzyx,xw->fwzy", fields, kernel_table, precision=lax.Precision.HIGHEST)
    return along_x.reshape(4, fields.shape[3], fields.shape[1] * fields.shape[2])


def fit_coeffs(smoothed):
    first, second, third, fourth = (smoothed[0], smoothed[1], smoothed[2], smoothed[3])
    inside_mean = first / (second + eps_fit)
    outside_mean = (third - first) / (1.0 - second + eps_fit)
    spread = fourth - third * third + eps_fit
    slope_term = 2.0 * (inside_mean - outside_mean) / spread
    offset = (outside_mean * outside_mean - inside_mean * inside_mean) / spread
    return jnp.stack([slope_term, offset])


def body(level_set, image):
    highest = lax.Precision.HIGHEST
    z_local, y_local, length = level_set.shape
    n_row = lax.axis_size("row")
    kernel_table = gauss_table(length)
    heaviside = 0.5 + jnp.arctan(level_set) / jnp.pi
    fields = jnp.stack([heaviside * image, heaviside, image, image * image])
    along_x = lines_along_x(fields, kernel_table)
    row_table = kernel_table.reshape(n_row, y_local, length)
    x_local = length // n_row
    received = lax.all_to_all(along_x, "row", split_axis=1, concat_axis=2, tiled=True)
    received = received.reshape(4, x_local, n_row, z_local, y_local)
    along_y = jnp.einsum("fwrzy,ryv->fwzv", received, row_table, precision=highest)
    received_z = lax.all_to_all(along_y, "col", split_axis=3, concat_axis=2, tiled=True)
    along_z = jnp.einsum("fxzy,zw->fxyw", received_z, kernel_table, precision=highest)
    coeffs = fit_coeffs(along_z)
    returned = lax.all_to_all(coeffs, "col", split_axis=3, concat_axis=2, tiled=True)
    returned = lax.all_to_all(returned, "row", split_axis=2, concat_axis=1, tiled=True)
    local_coeffs = jnp.transpose(returned, (0, 3, 2, 1))
    forcing = image * local_coeffs[0] + local_coeffs[1]
    padded = extended(level_set, (("row", 1), ("col", 0)), 1)
    laplace = (
        padded[2:, 1:-1, :]
        + padded[:-2, 1:-1, :]
        + padded[1:-1, 2:, :]
        + padded[1:-1, :-2, :]
        + jnp.roll(level_set, 1, 2)
        + jnp.roll(level_set, -1, 2)
        - 6.0 * level_set
    )
    dirac_weight = 1.0 / (jnp.pi * (1.0 + level_set * level_set))
    return level_set + dt_step * (nu_diff * laplace + dirac_weight * forcing)


def solution(mesh):
    return jax.shard_map(
        body,
        mesh=mesh,
        in_specs=(P("col", "row", None), P("col", "row", None)),
        out_specs=P("col", "row", None),
        check_vma=False,
    )
```

profile of v0, /device:TPU:0, one launch (start us, length us, event | category | flops | bytes accessed | tf_op | source)
XLA Modules:
  0.0 701.7 jit_solution(235425075818692739)
XLA Ops:
  0.0 0.6 fusion.59
  0.6 4.3 multiply_bitcast_fusion.1
  4.9 16.5 %fusion = f32[384,4,24,48]{0,3,2,1:T(8,128)} fusion(f32[1,24,48,384]{3,2,1,0:T(8,128)S(1)} %get-tuple-element.17, f32[1,24,48,384]{3,2,1,0:T(8,128)S(1)} %bitcast.87, f32[1,24,48,384]{3,2,1,0:T(8,128)S(1)} %get-tuple-element.16, f32[1,24,48,384]{3,2,1,0:T(8,128)S(1)} %get-tuple-element.15, f32[]{:T(128)} %fusion.59), kind=kOutput, calls=%fused_computation | convolution fusion | flops 8160804864 | bytes 14155780 | tf_op jit(solution)/shard_map/fzyx,xw->fwzy/dot_general | solution.py:48
  21.4 10.1 %copy.27 = f32[4,384,1152]{2,0,1:T(4,128)} copy(f32[4,384,1152]{1,2,0:T(8,128)} %bitcast.86) | data formatting | bytes 14155776 | tf_op jit(solution)/shard_map/reshape | solution.py:49
  31.5 6.6 all-to-all-start
  38.1 79.5 %all-to-all-done = f32[4,384,1152]{2,0,1:T(4,128)} async-done(((f32[4,384,1152]{2,0,1:T(4,128)}), f32[4,384,1152]{2,0,1:T(4,128)}, u32[]{:S(2)}, u32[]{:S(2)}) %all-to-all-start) | async-done | bytes 7077920 | tf_op jit(solution)/shard_map/all_to_all | solution.py:72
  117.6 3.5 copy.28
  121.0 5.1 copy.29
  126.1 15.1 %reshape.71 = f32[4,48,8,24,48]{4,3,2,1,0:T(8,128)} reshape(f32[4,48,8,1152]{3,2,1,0:T(8,128)} %copy.29) | data formatting | bytes 14155776 | tf_op jit(solution)/shard_map/reshape | solution.py:73
  141.2 22.0 %convolution_bitcast_fusion = f32[4,48,24,384]{3,2,1,0:T(8,128)} fusion(f32[4,48,8,24,48]{4,3,2,1,0:T(8,128)} %reshape.71, f32[]{:T(128)} %fusion.59, s32[8,48]{1,0:T(8,128)S(1)} %multiply_add_fusion.1), kind=kOutput, calls=%fused_computation.9 | convolution fusion | flops 8155496448 | bytes 14157316 | tf_op jit(solution)/shard_map/fwrzy,ryv->fwzv/dot_general | solution.py:74
  163.2 17.4 %copy.30 = f32[4,48,24,384]{1,2,0,3:T(8,128)} copy(f32[4,48,24,384]{3,2,1,0:T(8,128)} %convolution_bitcast_fusion) | data formatting | bytes 14155776 | tf_op jit(solution)/shard_map/fwrzy,ryv->fwzv/dot_general | solution.py:74
  180.6 22.5 %reshape.75 = f32[16,1,110592]{2,1,0:T(1,128)} reshape(f32[384,4,24,48]{3,2,1,0:T(8,128)} %bitcast.76) | data formatting | bytes 14155776
  203.1 89.9 %all_to_all.69 = f32[16,1,110592]{2,1,0:T(1,128)} all-to-all(f32[16,1,110592]{2,1,0:T(1,128)} %reshape.75), channel_id=1, replica_groups=mesh['row'=8,'col'=16] {'col'}, dimensions={0} | all-to-all | bytes 14155776 | tf_op jit(solution)/shard_map/all_to_all | solution.py:75
  293.1 0.6 broadcast.153
  293.6 76.7 %reduce = f32[16,110592]{1,0:T(8,128)} reduce(f32[16,1,110592]{2,1,0:T(1,128)} %all_to_all.69, f32[]{:T(128)} %broadcast.153), dimensions={1}, to_apply=%all_to_all.53.reduce_sub_computation | reduce | bytes 14155780 | tf_op jit(solution)/shard_map/all_to_all | solution.py:75
  370.3 18.8 %reshape.76 = f32[384,4,24,48]{3,2,1,0:T(8,128)} reshape(f32[16,110592]{1,0:T(8,128)} %reduce) | data formatting | bytes 14155776
  389.1 15.8 %copy.32 = f32[4,48,16,24,24]{1,4,3,2,0:T(8,128)} copy(f32[4,48,16,24,24]{1,3,0,4,2:T(8,128)} %bitcast.77) | data formatting | bytes 14155776 | tf_op jit(solution)/shard_map/all_to_all | solution.py:75
  404.9 14.5 %copy.33 = f32[4,48,384,24]{2,3,1,0:T(8,128)} copy(f32[4,48,384,24]{1,3,2,0:T(8,128)} %bitcast.78) | data formatting | bytes 14155776 | tf_op jit(solution)/shard_map/all_to_all | solution.py:75
  419.4 19.0 %fusion.38 = f32[4,48,24,384]{3,2,1,0:T(8,128)S(1)} fusion(f32[4,48,384,24]{2,3,1,0:T(8,128)} %copy.33, f32[]{:T(128)} %fusion.59), kind=kOutput, calls=%fused_computation.63 | convolution fusion | flops 8155496448 | bytes 14155780 | tf_op jit(solution)/shard_map/fxzy,zw->fxyw/dot_general | solution.py:76
  438.4 1.0 multiply_divide_fusion
  439.4 0.2 pad_maximum_fusion
  439.6 5.8 copy.34
  445.5 15.2 %reshape.77 = f32[16,1,55296]{2,1,0:T(1,128)} reshape(f32[384,2,24,48]{3,2,1,0:T(8,128)} %bitcast.79) | data formatting | bytes 7077888
  460.7 48.8 %all_to_all.70 = f32[16,1,55296]{2,1,0:T(1,128)S(1)} all-to-all(f32[16,1,55296]{2,1,0:T(1,128)} %reshape.77), channel_id=1, replica_groups=mesh['row'=8,'col'=16] {'col'}, dimensions={0} | all-to-all | bytes 7077888 | tf_op jit(solution)/shard_map/all_to_all | solution.py:78
  509.4 30.2 %reduce.1 = f32[16,55296]{1,0:T(8,128)} reduce(f32[16,1,55296]{2,1,0:T(1,128)S(1)} %all_to_all.70, f32[]{:T(128)} %broadcast.153), dimensions={1}, to_apply=%all_to_all.57.reduce_sub_computation | reduce | bytes 7077892 | tf_op jit(solution)/shard_map/all_to_all | solution.py:78
  539.7 11.1 %reshape.78 = f32[384,2,24,48]{3,2,1,0:T(8,128)} reshape(f32[16,55296]{1,0:T(8,128)} %reduce.1) | data formatting | bytes 7077888
  550.7 6.7 copy.36
  557.5 4.4 copy.48
  561.8 12.1 %reshape.79 = f32[8,1,110592]{2,1,0:T(1,128)} reshape(f32[384,2,24,48]{3,2,1,0:T(8,128)} %bitcast.82) | data formatting | bytes 7077888
  574.0 4.6 all-to-all-start.3
  578.6 0.1 fusion.75
  578.6 2.0 collective-permute-start
  580.6 2.3 collective-permute-start.1
  582.9 1.8 fusion.73
  584.6 37.2 %collective-permute-done = f32[24,1,384]{2,1,0:T(1,128)S(1)} collective-permute-done((f32[24,1,384]{2,1,0:T(1,128)S(1)}, f32[24,1,384]{2,1,0:T(1,128)S(1)}, u32[]{:S(2)}, u32[]{:S(2)}) %collective-permute-start) | collective-permute-done | bytes 36896 | tf_op jit(solution)/shard_map/ppermute | solution.py:22
  621.9 0.0 collective-permute-done.1
  621.9 0.6 copy-done.2
  622.5 0.7 pad_maximum_fusion.11
  623.2 0.7 collective-permute-start.2
  623.8 0.0 collective-permute-start.3
  623.8 1.2 fusion.74
  625.0 0.0 all-to-all-done.3
  625.1 39.6 %reduce.2 = f32[8,110592]{1,0:T(8,128)} reduce(f32[8,1,110592]{2,1,0:T(1,128)} %all-to-all-done.3, f32[]{:T(128)} %broadcast.153), dimensions={1}, to_apply=%all_to_all.61.reduce_sub_computation | reduce | bytes 7077892 | tf_op jit(solution)/shard_map/all_to_all | solution.py:79
  664.6 9.4 %reshape.80 = f32[384,2,24,48]{3,2,1,0:T(8,128)} reshape(f32[8,110592]{1,0:T(8,128)} %reduce.2) | data formatting | bytes 7077888
  674.1 12.8 %copy.39 = f32[2,8,48,48,24]{2,1,3,4,0:T(8,128)} copy(f32[2,8,48,48,24]{2,4,0,3,1:T(8,128)} %bitcast.83) | data formatting | bytes 7077888 | tf_op jit(solution)/shard_map/all_to_all | solution.py:79
  686.9 8.3 %all_to_all.64 = f32[2,384,48,24]{1,2,3,0:T(8,128)} reshape(f32[2,8,48,48,24]{2,1,3,4,0:T(8,128)} %copy.39) | data formatting | bytes 7077888 | tf_op jit(solution)/shard_map/all_to_all | solution.py:79
  695.1 0.0 collective-permute-done.2
  695.2 6.3 fusion.12
  (9 shorter events, 0.0 us)
Async XLA Ops:
  0.6 4.3 copy-start.1
  31.5 86.1 %all-to-all-start = ((f32[4,384,1152]{2,0,1:T(4,128)}), f32[4,384,1152]{2,0,1:T(4,128)}, u32[]{:S(2)}, u32[]{:S(2)}) async-start(f32[4,384,1152]{2,0,1:T(4,128)} %copy.27), calls=%async_computation | async-start | bytes 14155776 | tf_op jit(solution)/shard_map/all_to_all | solution.py:72
  574.0 4.6 copy-start
  574.0 51.1 %all-to-all-start.3 = ((f32[8,1,110592]{2,1,0:T(1,128)}), f32[8,1,110592]{2,1,0:T(1,128)}, u32[]{:S(2)}, u32[]{:S(2)}) async-start(f32[8,1,110592]{2,1,0:T(1,128)} %reshape.79), calls=%async_computation.3 | async-start | bytes 7077888 | tf_op jit(solution)/shard_map/all_to_all | solution.py:79
  578.6 43.2 %collective-permute-start = (f32[24,1,384]{2,1,0:T(1,128)S(1)}, f32[24,1,384]{2,1,0:T(1,128)S(1)}, u32[]{:S(2)}, u32[]{:S(2)}) collective-permute-start(f32[24,1,384]{2,1,0:T(1,128)S(1)} %get-tuple-element.14), channel_id=1, source_target_pairs={{0,16},{16,32},{32,48},{48,64},{64,80},{80,96},{96,112},{112,0},{1... | collective-permute-start | bytes 110600 | tf_op jit(solution)/shard_map/ppermute | solution.py:22
  580.6 41.3 %collective-permute-start.1 = (f32[24,1,384]{2,1,0:T(1,128)S(1)}, f32[24,1,384]{2,1,0:T(1,128)S(1)}, u32[]{:S(2)}, u32[]{:S(2)}) collective-permute-start(f32[24,1,384]{2,1,0:T(1,128)S(1)} %get-tuple-element.13), channel_id=1, source_target_pairs={{16,0},{32,16},{48,32},{64,48},{80,64},{96,80},{112,96},{0,112},{1... | collective-permute-start | bytes 110600 | tf_op jit(solution)/shard_map/ppermute | solution.py:23
  621.9 0.6 copy-start.2
  622.5 0.7 copy-start.3
  623.2 72.0 %collective-permute-start.2 = (f32[1,50,384]{2,1,0:T(8,128)}, f32[1,50,384]{2,1,0:T(8,128)}, u32[]{:S(2)}, u32[]{:S(2)}) collective-permute-start(f32[1,50,384]{2,1,0:T(8,128)} %get-tuple-element.7), channel_id=1, source_target_pairs={{1,0},{2,1},{3,2},{4,3},{5,4},{6,5},{7,6},{8,7},{9,8},{10,9},{11,1... | collective-permute-start | bytes 230408 | tf_op jit(solution)/shard_map/ppermute | solution.py:23
  623.8 71.3 %collective-permute-start.3 = (f32[1,50,384]{2,1,0:T(8,128)}, f32[1,50,384]{2,1,0:T(8,128)}, u32[]{:S(2)}, u32[]{:S(2)}) collective-permute-start(f32[1,50,384]{2,1,0:T(8,128)} %get-tuple-element.8), channel_id=1, source_target_pairs={{0,1},{1,2},{2,3},{3,4},{4,5},{5,6},{6,7},{7,8},{8,9},{9,10},{10,1... | collective-permute-start | bytes 230408 | tf_op jit(solution)/shard_map/ppermute | solution.py:22
where the time goes:
time: 715 us; the launch traced here: 702 us
  local copies, waits for them, and re-layouts  213 us (30%)
  other arithmetic  160 us (22%)
  blocking collectives  139 us (19%)
  waiting for transfers between devices  117 us (16%)
  matrix products  57.5 us (8%)
  starting transfers between devices  16.1 us (2%)
    all_to_all x1, blocking collectives, body(): lax.all_to_all(along_y, 'col', split_axis=3, concat_axis=2, tiled=True)  89.9 us
    unnamed x14, local copies, waits for them, and re-layouts  89.8 us
    all_to_all x1, waiting for transfers between devices, body(): lax.all_to_all(along_x, 'row', split_axis=1, concat_axis=2, tiled=True)  79.5 us
    all_to_all x1, other arithmetic, body(): lax.all_to_all(along_y, 'col', split_axis=3, concat_axis=2, tiled=True)  76.7 us
    all_to_all x1, blocking collectives, body(): lax.all_to_all(coeffs, 'col', split_axis=3, concat_axis=2, tiled=True)  48.8 us
    all_to_all x1, other arithmetic, body(): lax.all_to_all(returned, 'row', split_axis=2, concat_axis=1, tiled=True)  39.6 us
    ppermute x2, waiting for transfers between devices, extended(): before = lax.ppermute(last, axis, up)  37.2 us
    all_to_all x3, local copies, waits for them, and re-layouts, body(): lax.all_to_all(along_y, 'col', split_axis=3, concat_axis=2, tiled=True)  30.8 us
  transfers between devices with their start and end apart: 6, of which 2 were waited for; matrix products, arithmetic and copies ran while one was open for 9% of the time, Pallas kernels for 0%

commit v1 on v0

v1 whole, which is shorter than its diff:
```python
import functools

import jax
import jax.numpy as jnp
import ml_dtypes
import numpy as np
from jax import lax
from jax.experimental import pallas as pl
from jax.experimental.pallas import tpu as pltpu
from jax.sharding import PartitionSpec as P

R = 6
N = 384
ZL, YL = 24, 48
ZE, YE = ZL + 2 * R, YL + 16
EPS = 0.05
SIGMA = 8.0
DT, NU = 0.5, 0.1
G = 4
F32, BF16 = jnp.float32, jnp.bfloat16
MESH = pl.DeviceIdType.MESH

ATAN = (
    0.3183096647262573, -0.10609224438667297, 0.06349188834428787, -0.044272541999816895,
    0.03069206140935421, -0.0177974384278059, 0.006959190126508474, -0.0012906072661280632,
)


def taps():
    offsets = np.arange(-R, R + 1, dtype=np.float64)
    weights = np.exp(-offsets * offsets / (2.0 * SIGMA * SIGMA))
    return weights / weights.sum()


def split(table):
    high = table.astype(np.float32).astype(ml_dtypes.bfloat16)
    low = (table - high.astype(np.float64)).astype(np.float32).astype(ml_dtypes.bfloat16)
    return high, low


def tables():
    weights = taps()

    def tap(distance):
        return weights[R + distance] if abs(distance) <= R else 0.0

    centre = weights[R]
    source = list(range(YL)) + list(range(-8, 0)) + list(range(YL, YL + 8))

    def block(outs, cols):
        one = np.array([[tap(source[c] - o) * centre for c in cols] for o in outs])
        return np.kron(np.eye(G), one)

    inner = block(range(8, 40), range(YL))
    edge = block(list(range(8)) + list(range(40, 48)), range(YE))
    i = np.arange(N)
    d = np.abs(i[:, None] - i[None, :])
    d = np.minimum(d, N - d)
    along_x = np.where(d <= R, weights[np.minimum(R + d, 2 * R)], 0.0)
    return split(inner) + split(edge) + split(along_x)


def heaviside(level):
    size = jnp.abs(level)
    big = size > 1.0
    t = jnp.where(big, 1.0 / jnp.maximum(size, 1.0), size)
    u = t * t
    q = jnp.full_like(u, ATAN[-1])
    for coeff in ATAN[-2::-1]:
        q = q * u + coeff
    q = q * t
    q = jnp.where(big, 0.5 - q, q)
    return 0.5 + jnp.where(level < 0.0, -q, q)


def kernel(level_hbm, image_hbm, yi_h, yi_l, ye_h, ye_l, x_h, x_l, out_ref,
           lev, img, hv, hi, ii, g_h, g_l, xs_h, xs_l, sm,
           t_yih, t_yil, t_yeh, t_yel, t_xh, t_xl,
           local_sem, send_sem, recv_sem):
    row, col = lax.axis_index("row"), lax.axis_index("col")
    n_row, n_col = lax.axis_size("row"), lax.axis_size("col")
    r_up, r_dn = lax.rem(row + 1, n_row), lax.rem(row + n_row - 1, n_row)
    c_up, c_dn = lax.rem(col + 1, n_col), lax.rem(col + n_col - 1, n_col)

    barrier = pltpu.get_barrier_semaphore()
    around = [{"row": r, "col": c} for r in (r_dn, row, r_up) for c in (c_dn, col, c_up)]
    del around[4]
    for device in around:
        pl.semaphore_signal(barrier, inc=1, device_id=device, device_id_type=MESH)

    own = []
    for i, (src, dst) in enumerate((
        (level_hbm, lev.at[R:R + ZL, 0:YL]), (image_hbm, img.at[R:R + ZL, 0:YL]),
        (yi_h, t_yih), (yi_l, t_yil), (ye_h, t_yeh), (ye_l, t_yel), (x_h, t_xh), (x_l, t_xl),
    )):
        copy = pltpu.make_async_copy(src, dst, local_sem.at[i])
        copy.start()
        own.append(copy)

    pl.semaphore_wait(barrier, 8)

    z_src = {1: pl.ds(ZL - R, R), 0: pl.ds(0, ZL), -1: pl.ds(0, R)}
    z_dst = {1: pl.ds(0, R), 0: pl.ds(R, ZL), -1: pl.ds(R + ZL, R)}
    y_src = {1: pl.ds(YL - 8, 8), 0: pl.ds(0, YL), -1: pl.ds(0, 8)}
    y_dst = {1: pl.ds(YL, 8), 0: pl.ds(0, YL), -1: pl.ds(YL + 8, 8)}
    rows_of, cols_of = {1: r_up, 0: row, -1: r_dn}, {1: c_up, 0: col, -1: c_dn}
    remote = {}
    order = [(0, 1), (0, -1), (1, 0), (-1, 0), (1, 1), (1, -1), (-1, 1), (-1, -1)]
    for k, (dr, dc) in enumerate(order):
        for a, (src, dst) in enumerate(((level_hbm, lev), (image_hbm, img))):
            copy = pltpu.make_async_remote_copy(
                src_ref=src.at[z_src[dc], y_src[dr]],
                dst_ref=dst.at[z_dst[dc], y_dst[dr]],
                send_sem=send_sem.at[k, a],
                recv_sem=recv_sem.at[k, a],
                device_id={"row": rows_of[dr], "col": cols_of[dc]},
                device_id_type=MESH,
            )
            copy.start()
            remote[k, a] = copy

    def fields(first, count, start, size, step):
        @pl.loop(first, first + count)
        def _(p):
            for s in range(start, start + size, step):
                rows = slice(s, s + step)
                h = heaviside(lev[p, rows, :])
                im = img[p, rows, :]
                hv[p, rows, :] = h
                hi[p, rows, :] = h * im
                ii[p, rows, :] = im * im

    weights = taps()
    ratio = [float(np.float32(weights[R + d] / weights[R])) for d in range(R + 1)]

    def smooth_z(g, chunks):
        for k, ref in enumerate((hi, hv, img, ii)):
            for rc in chunks:
                rows = slice(rc * 16, rc * 16 + 16)
                for lt in range(3):
                    lanes = slice(lt * 128, lt * 128 + 128)
                    f = [ref[g * G + j, rows, lanes] for j in range(G + 2 * R)]
                    for o in range(G):
                        total = f[o + R]
                        for d in range(1, R + 1):
                            total = total + ratio[d] * (f[o + R - d] + f[o + R + d])
                        high = total.astype(BF16)
                        g_h[k, g * G + o, rows, lanes] = high
                        g_l[k, g * G + o, rows, lanes] = (total - high.astype(F32)).astype(BF16)

    def dot(a, b):
        return jnp.dot(a, b, preferred_element_type=F32)

    def finish(g, t_h, t_l, depth, rows_out):
        m = G * rows_out
        planes = pl.ds(g * G, G)
        for k in range(4):
            high = g_h[k, planes, 0:depth, :].reshape(G * depth, N)
            low = g_l[k, planes, 0:depth, :].reshape(G * depth, N)
            y = dot(t_h[...], high) + dot(t_l[...], high) + dot(t_h[...], low)
            yh = y.astype(BF16)
            xs_h[k * m:(k + 1) * m, :] = yh
            xs_l[k * m:(k + 1) * m, :] = (y - yh.astype(F32)).astype(BF16)
        a = xs_h[0:4 * m, :]
        sm[0:4 * m, :] = dot(a, t_xh[...]) + dot(a, t_xl[...]) + dot(xs_l[0:4 * m, :], t_xh[...])

    def pointwise(p, rows, s_rows, up, down):
        base, stride = s_rows
        s1, s2, s3, s4 = (sm[pl.ds(base + k * stride, rows.stop - rows.start), :] for k in range(4))
        level = lev[p + R, rows, :]
        im = img[p + R, rows, :]
        inner = s2 + EPS
        outer = 1.0 - s2 + EPS
        rest = s3 - s1
        both = inner * outer
        x1, x2 = s1 * outer, rest * inner
        spread = s4 - s3 * s3 + EPS
        force = (x1 - x2) * (2.0 * im * both - (x1 + x2)) / (both * both * spread * (np.pi * (1.0 + level * level)))
        lap = (lev[p + R + 1, rows, :] + lev[p + R - 1, rows, :] + up + down
               + pltpu.roll(level, 1, 1) + pltpu.roll(level, N - 1, 1) - 6.0 * level)
        out_ref[p, rows, :] = level + DT * (NU * lap + force)

    def inner_group(g):
        smooth_z(g, range(3))
        finish(g, t_yih, t_yil, YL, 32)

        @pl.loop(0, G)
        def _(o):
            p = g * G + o
            for s in range(8, 40, 8):
                pointwise(p, slice(s, s + 8), (o * 32 + s - 8, G * 32),
                          lev[p + R, s + 1:s + 9, :], lev[p + R, s - 1:s + 7, :])

    def edge_group(g):
        smooth_z(g, range(3, 4))
        finish(g, t_yeh, t_yel, YE, 16)

        @pl.loop(0, G)
        def _(o):
            p = g * G + o
            sub = lax.broadcasted_iota(jnp.int32, (8, N), 0)
            level = lev[p + R, 0:8, :]
            before = lev[p + R, YL:YL + 8, :]
            down = jnp.where(sub == 0, pltpu.roll(before, 1, 0), pltpu.roll(level, 1, 0))
            pointwise(p, slice(0, 8), (o * 16, G * 16), lev[p + R, 1:9, :], down)
            level = lev[p + R, 40:48, :]
            after = lev[p + R, YL + 8:YL + 16, :]
            up = jnp.where(sub == 7, pltpu.roll(after, 7, 0), pltpu.roll(level, 7, 0))
            pointwise(p, slice(40, 48), (o * 16 + 8, G * 16), up, lev[p + R, 39:47, :])

    for copy in own:
        copy.wait()
    fields(R, ZL, 0, YL, 16)
    pl.loop(2, 4)(inner_group)

    for k in (0, 1):
        for a in (0, 1):
            remote[k, a].wait_recv()
    fields(0, R, 0, YL, 16)
    fields(R + ZL, R, 0, YL, 16)
    pl.loop(0, 2)(inner_group)
    pl.loop(4, 6)(inner_group)

    for k in range(2, 8):
        for a in (0, 1):
            remote[k, a].wait_recv()
    fields(0, ZE, YL, 16, 16)
    pl.loop(0, 6)(edge_group)

    for k in range(8):
        for a in (0, 1):
            remote[k, a].wait_send()


def step(level_set, image):
    consts = [jnp.asarray(t) for t in tables()]
    ext = pltpu.VMEM((ZE, YE, N), F32)
    half = pltpu.VMEM((4, ZL, YE, N), BF16)
    rows = 4 * G * 32
    return pl.pallas_call(
        kernel,
        out_shape=jax.ShapeDtypeStruct((ZL, YL, N), F32),
        in_specs=[pl.BlockSpec(memory_space=pl.ANY)] * 8,
        out_specs=pl.BlockSpec(memory_space=pltpu.VMEM),
        scratch_shapes=[ext] * 5 + [half, half, pltpu.VMEM((rows, N), BF16), pltpu.VMEM((rows, N), BF16),
                                    pltpu.VMEM((rows, N), F32)]
        + [pltpu.VMEM(c.shape, BF16) for c in consts]
        + [pltpu.SemaphoreType.DMA((8,)), pltpu.SemaphoreType.DMA((8, 2)), pltpu.SemaphoreType.DMA((8, 2))],
        compiler_params=pltpu.CompilerParams(
            collective_id=0, has_side_effects=True, vmem_limit_bytes=48 * 1024 * 1024),
    )(level_set, image, *consts)


def solution(mesh):
    return jax.shard_map(
        step,
        mesh=mesh,
        in_specs=(P("col", "row", None), P("col", "row", None)),
        out_specs=P("col", "row", None),
        check_vma=False,
    )
```

time: 715 us -> 61.3 us (0.09); the launches traced: 702 us -> 60.9 us
  local copies, waits for them, and re-layouts: 213 us -> 9.28 us
  other arithmetic: 160 us -> 0 us
  blocking collectives: 139 us -> 0 us
  waiting for transfers between devices: 117 us -> 0 us
  matrix products: 57.5 us -> 0 us
  Pallas kernels: 0 us -> 51.6 us
  starting transfers between devices: 16.1 us -> 0 us
    all_to_all x3 -> x0, other arithmetic: 146 us -> none  [the longest x1 76.7 us: body(): lax.all_to_all(along_y, 'col', split_axis=3, concat_axis=2, tiled=True)]
    all_to_all x2 -> x0, blocking collectives: 139 us -> none  [the longest x1 89.9 us: body(): lax.all_to_all(along_y, 'col', split_axis=3, concat_axis=2, tiled=True)]
    unnamed x14 -> x17, local copies, waits for them, and re-layouts: 89.8 us -> 9.28 us
    all_to_all x2 -> x0, waiting for transfers between devices: 79.5 us -> none  [the longest x1 79.5 us: body(): lax.all_to_all(along_x, 'row', split_axis=1, concat_axis=2, tiled=True)]
    all_to_all x9 -> x0, local copies, waits for them, and re-layouts: 71.5 us -> none  [the longest x3 30.8 us: body(): lax.all_to_all(along_y, 'col', split_axis=3, concat_axis=2, tiled=True)]
    dot_general x3 -> x0, matrix products: 57.5 us -> none  [the longest x1 22 us: body(): jnp.einsum('fwrzy,ryv->fwzv', received, row_table, precision=highest)]
    pallas_call x0 -> x1, Pallas kernels: none -> 51.6 us  [step(): pl.pallas_call(kernel, out_shape=jax.ShapeDtypeStruct((ZL, YL, N), F32),...]
    ppermute x4 -> x0, waiting for transfers between devices: 37.2 us -> none  [the longest x2 37.2 us: extended(): before = lax.ppermute(last, axis, up)]
  transfers between devices with their start and end apart: 6 -> 0, of which waited for: 2 -> 0; matrix products, arithmetic and copies ran while one was open for 9% -> 0% of each run, Pallas kernels for 0% -> 0%
where the time goes in v1:
time: 61.3 us; the launch traced here: 60.9 us
  Pallas kernels  51.6 us (84%)
  local copies, waits for them, and re-layouts  9.28 us (15%)
    pallas_call x1, Pallas kernels, step(): pl.pallas_call(kernel, out_shape=jax.ShapeDtypeStruct((ZL, YL, N), F32),...  51.6 us
    unnamed x17, local copies, waits for them, and re-layouts  9.28 us

profile of v1, /device:TPU:0, one launch (start us, length us, event | category | flops | bytes accessed | tf_op | source)
XLA Modules:
  0.0 60.9 jit_solution(11763163445985858207)
XLA Ops:
  0.0 0.0 copy-start
  0.0 1.5 %copy-done = f32[24,48,384]{2,1,0:T(8,128)S(1)} copy-done((f32[24,48,384]{2,1,0:T(8,128)S(1)}, f32[24,48,384]{2,1,0:T(8,128)}, u32[]{:S(2)}) %copy-start) | copy-done | bytes 1769496
  1.5 0.0 copy-start.1
  1.5 1.5 %copy-done.1 = f32[24,48,384]{2,1,0:T(8,128)S(1)} copy-done((f32[24,48,384]{2,1,0:T(8,128)S(1)}, f32[24,48,384]{2,1,0:T(8,128)}, u32[]{:S(2)}) %copy-start.1) | copy-done | bytes 1769496
  3.0 0.0 copy-start.2
  3.0 1.0 %copy-done.2 = bf16[384,384]{1,0:T(8,128)(2,1)S(1)} copy-done((bf16[384,384]{1,0:T(8,128)(2,1)S(1)}, bf16[384,384]{1,0:T(8,128)(2,1)}, u32[]{:S(2)}) %copy-start.2) | copy-done | bytes 294936
  3.9 0.0 copy-start.3
  3.9 1.0 %copy-done.3 = bf16[384,384]{1,0:T(8,128)(2,1)S(1)} copy-done((bf16[384,384]{1,0:T(8,128)(2,1)S(1)}, bf16[384,384]{1,0:T(8,128)(2,1)}, u32[]{:S(2)}) %copy-start.3) | copy-done | bytes 294936
  4.9 0.0 copy-start.4
  4.9 0.8 %copy-done.4 = bf16[128,192]{1,0:T(8,128)(2,1)S(1)} copy-done((bf16[128,192]{1,0:T(8,128)(2,1)S(1)}, bf16[128,192]{1,0:T(8,128)(2,1)}, u32[]{:S(2)}) %copy-start.4) | copy-done | bytes 49176
  5.7 0.0 copy-start.5
  5.7 0.8 %copy-done.5 = bf16[128,192]{1,0:T(8,128)(2,1)S(1)} copy-done((bf16[128,192]{1,0:T(8,128)(2,1)S(1)}, bf16[128,192]{1,0:T(8,128)(2,1)}, u32[]{:S(2)}) %copy-start.5) | copy-done | bytes 49176
  6.6 0.0 copy-start.6
  6.6 0.8 %copy-done.6 = bf16[64,256]{1,0:T(8,128)(2,1)S(1)} copy-done((bf16[64,256]{1,0:T(8,128)(2,1)S(1)}, bf16[64,256]{1,0:T(8,128)(2,1)}, u32[]{:S(2)}) %copy-start.6) | copy-done | bytes 32792
  7.3 0.0 copy-start.7
  7.3 0.8 %copy-done.7 = bf16[64,256]{1,0:T(8,128)(2,1)S(1)} copy-done((bf16[64,256]{1,0:T(8,128)(2,1)S(1)}, bf16[64,256]{1,0:T(8,128)(2,1)}, u32[]{:S(2)}) %copy-start.7) | copy-done | bytes 32792
  8.1 51.6 %shard_map.82 = f32[24,48,384]{2,1,0:T(8,128)S(1)} custom-call(f32[24,48,384]{2,1,0:T(8,128)S(1)} %copy-done, f32[24,48,384]{2,1,0:T(8,128)S(1)} %copy-done.1, bf16[128,192]{1,0:T(8,128)(2,1)S(1)} %copy-done.5, bf16[128,192]{1,0:T(8,128)(2,1)S(1)} %copy-done.4, bf16[64,256]{1,0:T(8,128)(2,1)S(1)} %copy-done.7, bf16[64,256]{1,0:T(8,128)(2,1)S(1)} %copy-done.6, ...), custom_call_target="tpu_custom_call" | custom-call | tf_op jit(solution)/shard_map/pallas_call | solution.py:240
  59.7 1.2 %copy.10 = f32[24,48,384]{2,1,0:T(8,128)} copy(f32[24,48,384]{2,1,0:T(8,128)S(1)} %shard_map.82) | data formatting | bytes 3538944
Async XLA Ops:
  0.0 1.5 %copy-start = (f32[24,48,384]{2,1,0:T(8,128)S(1)}, f32[24,48,384]{2,1,0:T(8,128)}, u32[]{:S(2)}) copy-start(f32[24,48,384]{2,1,0:T(8,128)} %level_hbm.1) | copy-start | bytes 5308420
  1.5 1.5 %copy-start.1 = (f32[24,48,384]{2,1,0:T(8,128)S(1)}, f32[24,48,384]{2,1,0:T(8,128)}, u32[]{:S(2)}) copy-start(f32[24,48,384]{2,1,0:T(8,128)} %image_hbm.1) | copy-start | bytes 5308420
  3.0 1.0 %copy-start.2 = (bf16[384,384]{1,0:T(8,128)(2,1)S(1)}, bf16[384,384]{1,0:T(8,128)(2,1)}, u32[]{:S(2)}) copy-start(bf16[384,384]{1,0:T(8,128)(2,1)} %constant.17.clone.x_l) | copy-start | bytes 884740
  3.9 1.0 %copy-start.3 = (bf16[384,384]{1,0:T(8,128)(2,1)S(1)}, bf16[384,384]{1,0:T(8,128)(2,1)}, u32[]{:S(2)}) copy-start(bf16[384,384]{1,0:T(8,128)(2,1)} %constant.16.clone.x_h) | copy-start | bytes 884740
  4.9 0.8 %copy-start.4 = (bf16[128,192]{1,0:T(8,128)(2,1)S(1)}, bf16[128,192]{1,0:T(8,128)(2,1)}, u32[]{:S(2)}) copy-start(bf16[128,192]{1,0:T(8,128)(2,1)} %constant.13.clone.yi_l) | copy-start | bytes 147460
  5.7 0.8 %copy-start.5 = (bf16[128,192]{1,0:T(8,128)(2,1)S(1)}, bf16[128,192]{1,0:T(8,128)(2,1)}, u32[]{:S(2)}) copy-start(bf16[128,192]{1,0:T(8,128)(2,1)} %constant.12.clone.yi_h) | copy-start | bytes 147460
  6.6 0.8 %copy-start.6 = (bf16[64,256]{1,0:T(8,128)(2,1)S(1)}, bf16[64,256]{1,0:T(8,128)(2,1)}, u32[]{:S(2)}) copy-start(bf16[64,256]{1,0:T(8,128)(2,1)} %constant.15.clone.ye_l) | copy-start | bytes 98308
  7.3 0.8 %copy-start.7 = (bf16[64,256]{1,0:T(8,128)(2,1)S(1)}, bf16[64,256]{1,0:T(8,128)(2,1)}, u32[]{:S(2)}) copy-start(bf16[64,256]{1,0:T(8,128)(2,1)} %constant.14.clone.ye_h) | copy-start | bytes 98308

commit v2 on v1

--- a/solution.py
+++ b/solution.py
@@ -83,9 +83,7 @@
     c_up, c_dn = lax.rem(col + 1, n_col), lax.rem(col + n_col - 1, n_col)
 
     barrier = pltpu.get_barrier_semaphore()
-    around = [{"row": r, "col": c} for r in (r_dn, row, r_up) for c in (c_dn, col, c_up)]
-    del around[4]
-    for device in around:
+    for device in ({"row": row, "col": c_up}, {"row": row, "col": c_dn}, {"row": r_up, "col": col}, {"row": r_dn, "col": col}):
         pl.semaphore_signal(barrier, inc=1, device_id=device, device_id_type=MESH)
 
     own = []
@@ -97,27 +95,39 @@
         copy.start()
         own.append(copy)
 
-    pl.semaphore_wait(barrier, 8)
-
-    z_src = {1: pl.ds(ZL - R, R), 0: pl.ds(0, ZL), -1: pl.ds(0, R)}
-    z_dst = {1: pl.ds(0, R), 0: pl.ds(R, ZL), -1: pl.ds(R + ZL, R)}
-    y_src = {1: pl.ds(YL - 8, 8), 0: pl.ds(0, YL), -1: pl.ds(0, 8)}
-    y_dst = {1: pl.ds(YL, 8), 0: pl.ds(0, YL), -1: pl.ds(YL + 8, 8)}
-    rows_of, cols_of = {1: r_up, 0: row, -1: r_dn}, {1: c_up, 0: col, -1: c_dn}
-    remote = {}
-    order = [(0, 1), (0, -1), (1, 0), (-1, 0), (1, 1), (1, -1), (-1, 1), (-1, -1)]
-    for k, (dr, dc) in enumerate(order):
-        for a, (src, dst) in enumerate(((level_hbm, lev), (image_hbm, img))):
+    pl.semaphore_wait(barrier, 4)
+
+    sent = {}
+
+    def send(name, axis, target, src_level, src_image, dst):
+        for a, (src, to) in enumerate(((src_level, lev), (src_image, img))):
+            i = len(sent)
             copy = pltpu.make_async_remote_copy(
-                src_ref=src.at[z_src[dc], y_src[dr]],
-                dst_ref=dst.at[z_dst[dc], y_dst[dr]],
-                send_sem=send_sem.at[k, a],
-                recv_sem=recv_sem.at[k, a],
-                device_id={"row": rows_of[dr], "col": cols_of[dc]},
-                device_id_type=MESH,
+                src_ref=src, dst_ref=to.at[dst], send_sem=send_sem.at[i], recv_sem=recv_sem.at[i],
+                device_id={axis: target}, device_id_type=MESH,
             )
             copy.start()
-            remote[k, a] = copy
+            sent[name, a] = copy
+
+    def arrived(*parts):
+        for name in parts:
+            for a in (0, 1):
+                sent[name, a].wait_recv()
+
+    low, high, middle = pl.ds(0, R), pl.ds(ZL - R, R), pl.ds(R, ZL - 2 * R)
+    first_rows, last_rows = pl.ds(0, 8), pl.ds(YL - 8, 8)
+
+    def send_rows(name, planes, first):
+        for way, target, rows, to in ((0, r_up, last_rows, YL), (1, r_dn, first_rows, YL + 8)):
+            send((name, way), "row", target, level_hbm.at[planes, rows], image_hbm.at[planes, rows],
+                 (pl.ds(R + first, planes.size), pl.ds(to, 8)))
+
+    send_rows("low", low, 0)
+    send_rows("high", high, ZL - R)
+    own_rows = pl.ds(0, YL)
+    send("above", "col", c_up, level_hbm.at[high], image_hbm.at[high], (pl.ds(0, R), own_rows))
+    send("below", "col", c_dn, level_hbm.at[low], image_hbm.at[low], (pl.ds(R + ZL, R), own_rows))
+    send_rows("middle", middle, R)
 
     def fields(first, count, start, size, step):
         @pl.loop(first, first + count)
@@ -213,23 +223,25 @@
     fields(R, ZL, 0, YL, 16)
     pl.loop(2, 4)(inner_group)
 
-    for k in (0, 1):
-        for a in (0, 1):
-            remote[k, a].wait_recv()
+    arrived(("low", 0), ("low", 1), ("high", 0), ("high", 1))
+    halo_rows = pl.ds(YL, 16)
+    top, bottom = pl.ds(ZL, R), pl.ds(R, R)
+    send("corner above", "col", c_up, lev.at[top, halo_rows], img.at[top, halo_rows], (pl.ds(0, R), halo_rows))
+    send("corner below", "col", c_dn, lev.at[bottom, halo_rows], img.at[bottom, halo_rows],
+         (pl.ds(R + ZL, R), halo_rows))
+
+    arrived("above", "below")
     fields(0, R, 0, YL, 16)
     fields(R + ZL, R, 0, YL, 16)
     pl.loop(0, 2)(inner_group)
     pl.loop(4, 6)(inner_group)
 
-    for k in range(2, 8):
-        for a in (0, 1):
-            remote[k, a].wait_recv()
+    arrived(("middle", 0), ("middle", 1), "corner above", "corner below")
     fields(0, ZE, YL, 16, 16)
     pl.loop(0, 6)(edge_group)
 
-    for k in range(8):
-        for a in (0, 1):
-            remote[k, a].wait_send()
+    for copy in sent.values():
+        copy.wait_send()
 
 
 def step(level_set, image):
@@ -240,15 +252,15 @@
     return pl.pallas_call(
         kernel,
         out_shape=jax.ShapeDtypeStruct((ZL, YL, N), F32),
-        in_specs=[pl.BlockSpec(memory_space=pl.ANY)] * 8,
+        in_specs=[pl.BlockSpec(memory_space=pltpu.HBM)] * 8,
         out_specs=pl.BlockSpec(memory_space=pltpu.VMEM),
         scratch_shapes=[ext] * 5 + [half, half, pltpu.VMEM((rows, N), BF16), pltpu.VMEM((rows, N), BF16),
                                     pltpu.VMEM((rows, N), F32)]
         + [pltpu.VMEM(c.shape, BF16) for c in consts]
-        + [pltpu.SemaphoreType.DMA((8,)), pltpu.SemaphoreType.DMA((8, 2)), pltpu.SemaphoreType.DMA((8, 2))],
+        + [pltpu.SemaphoreType.DMA((8,)), pltpu.SemaphoreType.DMA((20,)), pltpu.SemaphoreType.DMA((20,))],
         compiler_params=pltpu.CompilerParams(
             collective_id=0, has_side_effects=True, vmem_limit_bytes=48 * 1024 * 1024),
-    )(level_set, image, *consts)
+    )(*[pltpu.with_memory_space_constraint(v, pltpu.HBM) for v in (level_set, image, *consts)])
 
 
 def solution(mesh):

time: 61.3 us -> 53.1 us (0.87)
  local copies, waits for them, and re-layouts: 9.28 us -> 1.21 us
    unnamed x17 -> x1, local copies, waits for them, and re-layouts: 9.28 us -> 1.21 us
where the time goes in v2:
time: 53.1 us; the launch traced here: 53 us
  Pallas kernels  51.7 us (97%)
  local copies, waits for them, and re-layouts  1.21 us (2%)
    pallas_call x1, Pallas kernels, step(): pl.pallas_call(kernel, out_shape=jax.ShapeDtypeStruct((ZL, YL, N), F32),...  51.7 us
    unnamed x1, local copies, waits for them, and re-layouts  1.21 us

profile of v2, /device:TPU:0, one launch (start us, length us, event | category | flops | bytes accessed | tf_op | source)
XLA Modules:
  0.0 53.0 jit_solution(10363659832604576922)
XLA Ops:
  0.0 51.7 %shard_map.82 = f32[24,48,384]{2,1,0:T(8,128)S(1)} custom-call(f32[24,48,384]{2,1,0:T(8,128)} %level_hbm.1, f32[24,48,384]{2,1,0:T(8,128)} %image_hbm.1, bf16[128,192]{1,0:T(8,128)(2,1)} %constant.12.clone.yi_h, bf16[128,192]{1,0:T(8,128)(2,1)} %constant.13.clone.yi_l, bf16[64,256]{1,0:T(8,128)(2,1)} %constant.14.clone.ye_h, ...), custom_call_target="tpu_custom_call" | custom-call | tf_op jit(solution)/shard_map/pallas_call | solution.py:252
  51.7 1.2 %copy.10 = f32[24,48,384]{2,1,0:T(8,128)} copy(f32[24,48,384]{2,1,0:T(8,128)S(1)} %shard_map.82) | data formatting | bytes 3538944

commit v3 on v2

--- a/solution.py
+++ b/solution.py
@@ -57,7 +57,7 @@
     d = np.abs(i[:, None] - i[None, :])
     d = np.minimum(d, N - d)
     along_x = np.where(d <= R, weights[np.minimum(R + d, 2 * R)], 0.0)
-    return split(inner) + split(edge) + split(along_x)
+    return tuple(np.concatenate(split(t)) for t in (inner, edge)) + split(along_x)
 
 
 def heaviside(level):
@@ -73,9 +73,9 @@
     return 0.5 + jnp.where(level < 0.0, -q, q)
 
 
-def kernel(level_hbm, image_hbm, yi_h, yi_l, ye_h, ye_l, x_h, x_l, out_ref,
+def kernel(level_hbm, image_hbm, y_in, y_ed, x_h, x_l, out_ref,
            lev, img, hv, hi, ii, g_h, g_l, xs_h, xs_l, sm,
-           t_yih, t_yil, t_yeh, t_yel, t_xh, t_xl,
+           t_yi, t_ye, t_xh, t_xl,
            local_sem, send_sem, recv_sem):
     row, col = lax.axis_index("row"), lax.axis_index("col")
     n_row, n_col = lax.axis_size("row"), lax.axis_size("col")
@@ -89,7 +89,7 @@
     own = []
     for i, (src, dst) in enumerate((
         (level_hbm, lev.at[R:R + ZL, 0:YL]), (image_hbm, img.at[R:R + ZL, 0:YL]),
-        (yi_h, t_yih), (yi_l, t_yil), (ye_h, t_yeh), (ye_l, t_yel), (x_h, t_xh), (x_l, t_xl),
+        (y_in, t_yi), (y_ed, t_ye), (x_h, t_xh), (x_l, t_xl),
     )):
         copy = pltpu.make_async_copy(src, dst, local_sem.at[i])
         copy.start()
@@ -99,14 +99,15 @@
 
     sent = {}
 
-    def send(name, axis, target, src_level, src_image, dst):
+    def send(name, axis, target, src_level, src_image, dst, now=True):
         for a, (src, to) in enumerate(((src_level, lev), (src_image, img))):
             i = len(sent)
             copy = pltpu.make_async_remote_copy(
                 src_ref=src, dst_ref=to.at[dst], send_sem=send_sem.at[i], recv_sem=recv_sem.at[i],
                 device_id={axis: target}, device_id_type=MESH,
             )
-            copy.start()
+            if now:
+                copy.start()
             sent[name, a] = copy
 
     def arrived(*parts):
@@ -124,10 +125,15 @@
 
     send_rows("low", low, 0)
     send_rows("high", high, ZL - R)
+    send_rows("middle", middle, R)
     own_rows = pl.ds(0, YL)
     send("above", "col", c_up, level_hbm.at[high], image_hbm.at[high], (pl.ds(0, R), own_rows))
     send("below", "col", c_dn, level_hbm.at[low], image_hbm.at[low], (pl.ds(R + ZL, R), own_rows))
-    send_rows("middle", middle, R)
+    halo_rows = pl.ds(YL, 16)
+    top, bottom = pl.ds(ZL, R), pl.ds(R, R)
+    send("corner above", "col", c_up, lev.at[top, halo_rows], img.at[top, halo_rows], (pl.ds(0, R), halo_rows), False)
+    send("corner below", "col", c_dn, lev.at[bottom, halo_rows], img.at[bottom, halo_rows],
+         (pl.ds(R + ZL, R), halo_rows), False)
 
     def fields(first, count, start, size, step):
         @pl.loop(first, first + count)
@@ -143,40 +149,41 @@
     weights = taps()
     ratio = [float(np.float32(weights[R + d] / weights[R])) for d in range(R + 1)]
 
-    def smooth_z(g, chunks):
+    def smooth_z(g, chunk):
+        rows = slice(chunk * 16, chunk * 16 + 16)
         for k, ref in enumerate((hi, hv, img, ii)):
-            for rc in chunks:
-                rows = slice(rc * 16, rc * 16 + 16)
-                for lt in range(3):
-                    lanes = slice(lt * 128, lt * 128 + 128)
-                    f = [ref[g * G + j, rows, lanes] for j in range(G + 2 * R)]
-                    for o in range(G):
-                        total = f[o + R]
-                        for d in range(1, R + 1):
-                            total = total + ratio[d] * (f[o + R - d] + f[o + R + d])
-                        high = total.astype(BF16)
-                        g_h[k, g * G + o, rows, lanes] = high
-                        g_l[k, g * G + o, rows, lanes] = (total - high.astype(F32)).astype(BF16)
+            for lt in range(3):
+                lanes = slice(lt * 128, lt * 128 + 128)
+                f = [ref[g * G + j, rows, lanes] for j in range(G + 2 * R)]
+                for o in range(G):
+                    total = f[o + R]
+                    for d in range(1, R + 1):
+                        total = total + ratio[d] * (f[o + R - d] + f[o + R + d])
+                    high = total.astype(BF16)
+                    g_h[k, g * G + o, rows, lanes] = high
+                    g_l[k, g * G + o, rows, lanes] = (total - high.astype(F32)).astype(BF16)
 
     def dot(a, b):
         return jnp.dot(a, b, preferred_element_type=F32)
 
-    def finish(g, t_h, t_l, depth, rows_out):
-        m = G * rows_out
+    def smooth_y(g, table, depth, base):
         planes = pl.ds(g * G, G)
+        m = table.shape[0] // 2
         for k in range(4):
             high = g_h[k, planes, 0:depth, :].reshape(G * depth, N)
             low = g_l[k, planes, 0:depth, :].reshape(G * depth, N)
-            y = dot(t_h[...], high) + dot(t_l[...], high) + dot(t_h[...], low)
+            y = dot(table[...], high)
+            y = y[0:m] + y[m:2 * m] + dot(table[0:m, :], low)
             yh = y.astype(BF16)
-            xs_h[k * m:(k + 1) * m, :] = yh
-            xs_l[k * m:(k + 1) * m, :] = (y - yh.astype(F32)).astype(BF16)
-        a = xs_h[0:4 * m, :]
-        sm[0:4 * m, :] = dot(a, t_xh[...]) + dot(a, t_xl[...]) + dot(xs_l[0:4 * m, :], t_xh[...])
-
-    def pointwise(p, rows, s_rows, up, down):
-        base, stride = s_rows
-        s1, s2, s3, s4 = (sm[pl.ds(base + k * stride, rows.stop - rows.start), :] for k in range(4))
+            xs_h[k * 128 + base:k * 128 + base + m, :] = yh
+            xs_l[k * 128 + base:k * 128 + base + m, :] = (y - yh.astype(F32)).astype(BF16)
+
+    def smooth_x():
+        a = xs_h[...]
+        sm[...] = dot(a, t_xh[...]) + dot(a, t_xl[...]) + dot(xs_l[...], t_xh[...])
+
+    def pointwise(p, rows, base, up, down):
+        s1, s2, s3, s4 = (sm[base + k * 128:base + k * 128 + 8, :] for k in range(4))
         level = lev[p + R, rows, :]
         im = img[p + R, rows, :]
         inner = s2 + EPS
@@ -190,55 +197,86 @@
                + pltpu.roll(level, 1, 1) + pltpu.roll(level, N - 1, 1) - 6.0 * level)
         out_ref[p, rows, :] = level + DT * (NU * lap + force)
 
-    def inner_group(g):
-        smooth_z(g, range(3))
-        finish(g, t_yih, t_yil, YL, 32)
-
-        @pl.loop(0, G)
-        def _(o):
+    def inner_points(g):
+        for o in range(G):
             p = g * G + o
             for s in range(8, 40, 8):
-                pointwise(p, slice(s, s + 8), (o * 32 + s - 8, G * 32),
-                          lev[p + R, s + 1:s + 9, :], lev[p + R, s - 1:s + 7, :])
-
-    def edge_group(g):
-        smooth_z(g, range(3, 4))
-        finish(g, t_yeh, t_yel, YE, 16)
-
-        @pl.loop(0, G)
-        def _(o):
-            p = g * G + o
-            sub = lax.broadcasted_iota(jnp.int32, (8, N), 0)
-            level = lev[p + R, 0:8, :]
-            before = lev[p + R, YL:YL + 8, :]
-            down = jnp.where(sub == 0, pltpu.roll(before, 1, 0), pltpu.roll(level, 1, 0))
-            pointwise(p, slice(0, 8), (o * 16, G * 16), lev[p + R, 1:9, :], down)
-            level = lev[p + R, 40:48, :]
-            after = lev[p + R, YL + 8:YL + 16, :]
-            up = jnp.where(sub == 7, pltpu.roll(after, 7, 0), pltpu.roll(level, 7, 0))
-            pointwise(p, slice(40, 48), (o * 16 + 8, G * 16), up, lev[p + R, 39:47, :])
+                pointwise(p, slice(s, s + 8), o * 32 + s - 8, lev[p + R, s + 1:s + 9, :], lev[p + R, s - 1:s + 7, :])
+
+    sub = lax.broadcasted_iota(jnp.int32, (8, N), 0)
+
+    def edge_points(e):
+        for o in range(2 * G):
+            p = e * 2 * G + o
+            down = jnp.where(sub == 0, pltpu.roll(lev[p + R, YL:YL + 8, :], 1, 0), pltpu.roll(lev[p + R, 0:8, :], 1, 0))
+            pointwise(p, slice(0, 8), o * 16, lev[p + R, 1:9, :], down)
+            up = jnp.where(sub == 7, pltpu.roll(lev[p + R, YL + 8:YL + 16, :], 7, 0),
+                           pltpu.roll(lev[p + R, 40:48, :], 7, 0))
+            pointwise(p, slice(40, 48), o * 16 + 8, up, lev[p + R, 39:47, :])
+
+    def inner(g):
+        for chunk in range(3):
+            smooth_z(g, chunk)
+        smooth_y(g, t_yi, YL, 0)
+        smooth_x()
+        inner_points(g)
+
+    def edge(e):
+        for half in range(2):
+            smooth_z(2 * e + half, 3)
+            smooth_y(2 * e + half, t_ye, YE, half * 64)
+        smooth_x()
+        edge_points(e)
+
+    even = lax.rem(col, 2) == 0
+    near = jnp.where(even, 1, 0)
+    far = 1 - near
+
+    def arrived_side(side, *parts):
+        for way, suffix in ((0, "above"), (1, "below")):
+            @pl.when(side == way)
+            def _():
+                arrived(*(part + suffix for part in parts))
 
     for copy in own:
         copy.wait()
     fields(R, ZL, 0, YL, 16)
-    pl.loop(2, 4)(inner_group)
+
+    @pl.loop(0, 4)
+    def _(i):
+        @pl.when(i == 2)
+        def _():
+            arrived_side(near, "")
+            fields(near * (R + ZL), R, 0, YL, 16)
+
+        inner(jnp.where(i < 2, i + 2, near * 4 + i - 2))
 
     arrived(("low", 0), ("low", 1), ("high", 0), ("high", 1))
-    halo_rows = pl.ds(YL, 16)
-    top, bottom = pl.ds(ZL, R), pl.ds(R, R)
-    send("corner above", "col", c_up, lev.at[top, halo_rows], img.at[top, halo_rows], (pl.ds(0, R), halo_rows))
-    send("corner below", "col", c_dn, lev.at[bottom, halo_rows], img.at[bottom, halo_rows],
-         (pl.ds(R + ZL, R), halo_rows))
-
-    arrived("above", "below")
-    fields(0, R, 0, YL, 16)
-    fields(R + ZL, R, 0, YL, 16)
-    pl.loop(0, 2)(inner_group)
-    pl.loop(4, 6)(inner_group)
-
-    arrived(("middle", 0), ("middle", 1), "corner above", "corner below")
-    fields(0, ZE, YL, 16, 16)
-    pl.loop(0, 6)(edge_group)
+    for name in ("corner above", "corner below"):
+        for a in (0, 1):
+            sent[name, a].start()
+    arrived(("middle", 0), ("middle", 1))
+    fields(R, ZL, YL, 16, 16)
+
+    @pl.loop(0, 2)
+    def _(i):
+        @pl.when(i == 1)
+        def _():
+            arrived_side(near, "corner ")
+            fields(near * (R + ZL), R, YL, 16, 16)
+
+        edge(jnp.where(i == 0, 1, near * 2))
+
+    arrived_side(far, "")
+    fields(far * (R + ZL), R, 0, YL, 16)
+
+    @pl.loop(0, 2)
+    def _(i):
+        inner(far * 4 + i)
+
+    arrived_side(far, "corner ")
+    fields(far * (R + ZL), R, YL, 16, 16)
+    edge(far * 2)
 
     for copy in sent.values():
         copy.wait_send()
@@ -252,7 +290,7 @@
     return pl.pallas_call(
         kernel,
         out_shape=jax.ShapeDtypeStruct((ZL, YL, N), F32),
-        in_specs=[pl.BlockSpec(memory_space=pltpu.HBM)] * 8,
+        in_specs=[pl.BlockSpec(memory_space=pltpu.HBM)] * 6,
         out_specs=pl.BlockSpec(memory_space=pltpu.VMEM),
         scratch_shapes=[ext] * 5 + [half, half, pltpu.VMEM((rows, N), BF16), pltpu.VMEM((rows, N), BF16),
                                     pltpu.VMEM((rows, N), F32)]

time: 53.1 us -> 42.2 us (0.79)
  Pallas kernels: 51.7 us -> 40.9 us
    pallas_call x1, Pallas kernels: 51.7 us -> 40.9 us  [step(): pl.pallas_call(kernel, out_shape=jax.ShapeDtypeStruct((ZL, YL, N), F32),...]
where the time goes in v3:
time: 42.2 us; the launch traced here: 42.1 us
  Pallas kernels  40.9 us (97%)
  local copies, waits for them, and re-layouts  1.21 us (3%)
    pallas_call x1, Pallas kernels, step(): pl.pallas_call(kernel, out_shape=jax.ShapeDtypeStruct((ZL, YL, N), F32),...  40.9 us
    unnamed x1, local copies, waits for them, and re-layouts  1.21 us

profile of v3, /device:TPU:0, one launch (start us, length us, event | category | flops | bytes accessed | tf_op | source)
XLA Modules:
  0.0 42.1 jit_solution(11814417881431320121)
XLA Ops:
  0.0 40.9 %shard_map.64 = f32[24,48,384]{2,1,0:T(8,128)S(1)} custom-call(f32[24,48,384]{2,1,0:T(8,128)} %level_hbm.1, f32[24,48,384]{2,1,0:T(8,128)} %image_hbm.1, bf16[256,192]{1,0:T(8,128)(2,1)} %constant.8.clone.y_in, bf16[128,256]{1,0:T(8,128)(2,1)} %constant.9.clone.y_ed, bf16[384,384]{1,0:T(8,128)(2,1)} %constant.10.clone.x_h, bf16[384,384]{1,0:T(8,128)(2,1)} %constant.11.clone.x_l), custom_call_target="tpu_custom_call" | custom-call | tf_op jit(solution)/shard_map/pallas_call | solution.py:290
  40.9 1.2 %copy.8 = f32[24,48,384]{2,1,0:T(8,128)} copy(f32[24,48,384]{2,1,0:T(8,128)S(1)} %shard_map.64) | data formatting | bytes 3538944

commit v4 on v3

--- a/solution.py
+++ b/solution.py
@@ -1,4 +1,4 @@
-import functools
+import typing
 
 import jax
 import jax.numpy as jnp
@@ -24,6 +24,17 @@
     0.3183096647262573, -0.10609224438667297, 0.06349188834428787, -0.044272541999816895,
     0.03069206140935421, -0.0177974384278059, 0.006959190126508474, -0.0012906072661280632,
 )
+
+
+class Part(typing.NamedTuple):
+    plane: int
+    planes: int
+    start: int
+    size: int
+
+
+PARTS = {"low": Part(0, R, 0, 40), "high": Part(ZL - R, R, 40, 40), "middle": Part(R, ZL - 2 * R, 80, 72)}
+PACKED = 152
 
 
 def taps():
@@ -76,7 +87,7 @@
 def kernel(level_hbm, image_hbm, y_in, y_ed, x_h, x_l, out_ref,
            lev, img, hv, hi, ii, g_h, g_l, xs_h, xs_l, sm,
            t_yi, t_ye, t_xh, t_xl,
-           local_sem, send_sem, recv_sem):
+           packed, halo, corner, local_sem, send_sem, recv_sem):
     row, col = lax.axis_index("row"), lax.axis_index("col")
     n_row, n_col = lax.axis_size("row"), lax.axis_size("col")
     r_up, r_dn = lax.rem(row + 1, n_row), lax.rem(row + n_row - 1, n_row)
@@ -95,45 +106,68 @@
         copy.start()
         own.append(copy)
 
+    for block in (lev, img):
+        block[:, YL:YE, :] = jnp.zeros((ZE, YE - YL, N), F32)
+    for side in (0, 1):
+        for a in (0, 1):
+            for part in PARTS.values():
+                if part.size > 6 * part.planes:
+                    packed[side, a, part.start + 6 * part.planes:part.start + part.size, :] = jnp.zeros(
+                        (part.size - 6 * part.planes, N), F32)
+
+    def pack(part):
+        for side, first in ((0, YL - R), (1, 0)):
+            for a, block in enumerate((lev, img)):
+                for q in range(part.planes):
+                    at = part.start + 6 * q
+                    packed[side, a, at:at + 6, :] = block[R + part.plane + q, first:first + 6, :]
+
+    def unpack(src, start, planes, to):
+        for side in (0, 1):
+            for a, block in enumerate((lev, img)):
+                for q in range(planes):
+                    at = start + 6 * q
+                    row0 = YL + 2 + 6 * side
+                    block[to + q, row0:row0 + 6, :] = src[side, a, at:at + 6, :]
+
+    sent = {}
+
+    def send(name, axis, target, src, dst, now=True):
+        i = len(sent)
+        copy = pltpu.make_async_remote_copy(
+            src_ref=src, dst_ref=dst, send_sem=send_sem.at[i], recv_sem=recv_sem.at[i],
+            device_id={axis: target}, device_id_type=MESH,
+        )
+        if now:
+            copy.start()
+        sent[name] = copy
+
+    def arrived(*names):
+        for name in names:
+            sent[name].wait_recv()
+
+    def send_part(name):
+        part = PARTS[name]
+        rows = pl.ds(part.start, part.size)
+        for side, target in ((0, r_up), (1, r_dn)):
+            send((name, side), "row", target, packed.at[side, :, rows], halo.at[side, :, rows])
+
+    own[0].wait()
+    own[1].wait()
+    pack(PARTS["low"])
+    pack(PARTS["high"])
     pl.semaphore_wait(barrier, 4)
-
-    sent = {}
-
-    def send(name, axis, target, src_level, src_image, dst, now=True):
-        for a, (src, to) in enumerate(((src_level, lev), (src_image, img))):
-            i = len(sent)
-            copy = pltpu.make_async_remote_copy(
-                src_ref=src, dst_ref=to.at[dst], send_sem=send_sem.at[i], recv_sem=recv_sem.at[i],
-                device_id={axis: target}, device_id_type=MESH,
-            )
-            if now:
-                copy.start()
-            sent[name, a] = copy
-
-    def arrived(*parts):
-        for name in parts:
-            for a in (0, 1):
-                sent[name, a].wait_recv()
-
-    low, high, middle = pl.ds(0, R), pl.ds(ZL - R, R), pl.ds(R, ZL - 2 * R)
-    first_rows, last_rows = pl.ds(0, 8), pl.ds(YL - 8, 8)
-
-    def send_rows(name, planes, first):
-        for way, target, rows, to in ((0, r_up, last_rows, YL), (1, r_dn, first_rows, YL + 8)):
-            send((name, way), "row", target, level_hbm.at[planes, rows], image_hbm.at[planes, rows],
-                 (pl.ds(R + first, planes.size), pl.ds(to, 8)))
-
-    send_rows("low", low, 0)
-    send_rows("high", high, ZL - R)
-    send_rows("middle", middle, R)
-    own_rows = pl.ds(0, YL)
-    send("above", "col", c_up, level_hbm.at[high], image_hbm.at[high], (pl.ds(0, R), own_rows))
-    send("below", "col", c_dn, level_hbm.at[low], image_hbm.at[low], (pl.ds(R + ZL, R), own_rows))
-    halo_rows = pl.ds(YL, 16)
-    top, bottom = pl.ds(ZL, R), pl.ds(R, R)
-    send("corner above", "col", c_up, lev.at[top, halo_rows], img.at[top, halo_rows], (pl.ds(0, R), halo_rows), False)
-    send("corner below", "col", c_dn, lev.at[bottom, halo_rows], img.at[bottom, halo_rows],
-         (pl.ds(R + ZL, R), halo_rows), False)
+    send_part("low")
+    send_part("high")
+    pack(PARTS["middle"])
+    send_part("middle")
+    low, high, own_rows = pl.ds(0, R), pl.ds(ZL - R, R), pl.ds(0, YL)
+    for a, (src, dst) in enumerate(((level_hbm, lev), (image_hbm, img))):
+        send(("above", a), "col", c_up, src.at[high], dst.at[pl.ds(0, R), own_rows])
+        send(("below", a), "col", c_dn, src.at[low], dst.at[pl.ds(R + ZL, R), own_rows])
+    outer = {"corner above": (c_up, PARTS["high"], 0), "corner below": (c_dn, PARTS["low"], 1)}
+    for name, (target, part, way) in outer.items():
+        send(name, "col", target, halo.at[:, :, pl.ds(part.start, part.size)], corner.at[way], False)
 
     def fields(first, count, start, size, step):
         @pl.loop(first, first + count)
@@ -232,50 +266,56 @@
     near = jnp.where(even, 1, 0)
     far = 1 - near
 
-    def arrived_side(side, *parts):
-        for way, suffix in ((0, "above"), (1, "below")):
+    def z_halo(side):
+        for way, name in ((0, "above"), (1, "below")):
             @pl.when(side == way)
             def _():
-                arrived(*(part + suffix for part in parts))
-
-    for copy in own:
+                arrived((name, 0), (name, 1))
+        fields(side * (R + ZL), R, 0, YL, 16)
+
+    def corner_halo(side):
+        for way, name in ((0, "corner above"), (1, "corner below")):
+            @pl.when(side == way)
+            def _():
+                arrived(name)
+                unpack(corner.at[way], 0, R, way * (R + ZL))
+        fields(side * (R + ZL), R, YL, 16, 16)
+
+    fields(R, ZL, 0, YL, 16)
+    for copy in own[2:]:
         copy.wait()
-    fields(R, ZL, 0, YL, 16)
 
     @pl.loop(0, 4)
     def _(i):
         @pl.when(i == 2)
         def _():
-            arrived_side(near, "")
-            fields(near * (R + ZL), R, 0, YL, 16)
+            z_halo(near)
 
         inner(jnp.where(i < 2, i + 2, near * 4 + i - 2))
 
     arrived(("low", 0), ("low", 1), ("high", 0), ("high", 1))
-    for name in ("corner above", "corner below"):
-        for a in (0, 1):
-            sent[name, a].start()
+    for name in outer:
+        sent[name].start()
     arrived(("middle", 0), ("middle", 1))
+    for part in PARTS.values():
+        unpack(halo, part.start, part.planes, R + part.plane)
     fields(R, ZL, YL, 16, 16)
 
     @pl.loop(0, 2)
     def _(i):
         @pl.when(i == 1)
         def _():
-            arrived_side(near, "corner ")
-            fields(near * (R + ZL), R, YL, 16, 16)
+            corner_halo(near)
 
         edge(jnp.where(i == 0, 1, near * 2))
 
-    arrived_side(far, "")
-    fields(far * (R + ZL), R, 0, YL, 16)
+    z_halo(far)
 
     @pl.loop(0, 2)
     def _(i):
         inner(far * 4 + i)
 
-    arrived_side(far, "corner ")
-    fields(far * (R + ZL), R, YL, 16, 16)
+    corner_halo(far)
     edge(far * 2)
 
     for copy in sent.values():
@@ -295,7 +335,8 @@
         scratch_shapes=[ext] * 5 + [half, half, pltpu.VMEM((rows, N), BF16), pltpu.VMEM((rows, N), BF16),
                                     pltpu.VMEM((rows, N), F32)]
         + [pltpu.VMEM(c.shape, BF16) for c in consts]
-        + [pltpu.SemaphoreType.DMA((8,)), pltpu.SemaphoreType.DMA((20,)), pltpu.SemaphoreType.DMA((20,))],
+        + [pltpu.VMEM((2, 2, PACKED, N), F32)] * 2 + [pltpu.VMEM((2, 2, 2, 40, N), F32)]
+        + [pltpu.SemaphoreType.DMA((8,)), pltpu.SemaphoreType.DMA((12,)), pltpu.SemaphoreType.DMA((12,))],
         compiler_params=pltpu.CompilerParams(
             collective_id=0, has_side_effects=True, vmem_limit_bytes=48 * 1024 * 1024),
     )(*[pltpu.with_memory_space_constraint(v, pltpu.HBM) for v in (level_set, image, *consts)])

time: 42.2 us -> 39.3 us (0.931)
  Pallas kernels: 40.9 us -> 38 us
    pallas_call x1, Pallas kernels: 40.9 us -> 38 us  [step(): pl.pallas_call(kernel, out_shape=jax.ShapeDtypeStruct((ZL, YL, N), F32),...]
where the time goes in v4:
time: 39.3 us; the launch traced here: 39.2 us
  Pallas kernels  38 us (97%)
  local copies, waits for them, and re-layouts  1.21 us (3%)
    pallas_call x1, Pallas kernels, step(): pl.pallas_call(kernel, out_shape=jax.ShapeDtypeStruct((ZL, YL, N), F32),...  38 us
    unnamed x1, local copies, waits for them, and re-layouts  1.21 us

profile of v4, /device:TPU:0, one launch (start us, length us, event | category | flops | bytes accessed | tf_op | source)
XLA Modules:
  0.0 39.2 jit_solution(15119435823905311490)
XLA Ops:
  0.0 38.0 %shard_map.64 = f32[24,48,384]{2,1,0:T(8,128)S(1)} custom-call(f32[24,48,384]{2,1,0:T(8,128)} %level_hbm.1, f32[24,48,384]{2,1,0:T(8,128)} %image_hbm.1, bf16[256,192]{1,0:T(8,128)(2,1)} %constant.8.clone.y_in, bf16[128,256]{1,0:T(8,128)(2,1)} %constant.9.clone.y_ed, bf16[384,384]{1,0:T(8,128)(2,1)} %constant.10.clone.x_h, bf16[384,384]{1,0:T(8,128)(2,1)} %constant.11.clone.x_l), custom_call_target="tpu_custom_call" | custom-call | tf_op jit(solution)/shard_map/pallas_call | solution.py:330
  38.0 1.2 %copy.8 = f32[24,48,384]{2,1,0:T(8,128)} copy(f32[24,48,384]{2,1,0:T(8,128)S(1)} %shard_map.64) | data formatting | bytes 3538944

commit v5 on v4

--- a/solution.py
+++ b/solution.py
@@ -1,3 +1,4 @@
+import functools
 import typing
 
 import jax
@@ -35,6 +36,7 @@
 
 PARTS = {"low": Part(0, R, 0, 40), "high": Part(ZL - R, R, 40, 40), "middle": Part(R, ZL - 2 * R, 80, 72)}
 PACKED = 152
+WINDOWS = (-32, 160)
 
 
 def taps():
@@ -64,11 +66,15 @@
 
     inner = block(range(8, 40), range(YL))
     edge = block(list(range(8)) + list(range(40, 48)), range(YE))
-    i = np.arange(N)
-    d = np.abs(i[:, None] - i[None, :])
-    d = np.minimum(d, N - d)
-    along_x = np.where(d <= R, weights[np.minimum(R + d, 2 * R)], 0.0)
-    return tuple(np.concatenate(split(t)) for t in (inner, edge)) + split(along_x)
+    halves = []
+    for start, first, outs in ((WINDOWS[0], 0, range(0, N // 2)), (WINDOWS[1], 128, range(N // 2, N))):
+        half = np.zeros((256, 256))
+        for o in outs:
+            for d in range(-R, R + 1):
+                half[o + d - start, o - first] = weights[R + d]
+        high, low = split(half)
+        halves.append(np.concatenate([high, high, low]))
+    return tuple(np.concatenate(split(t)) for t in (inner, edge)) + (np.stack(halves),)
 
 
 def heaviside(level):
@@ -84,10 +90,10 @@
     return 0.5 + jnp.where(level < 0.0, -q, q)
 
 
-def kernel(level_hbm, image_hbm, y_in, y_ed, x_h, x_l, out_ref,
+def kernel(level_hbm, image_hbm, y_in, y_ed, x_all, out_ref,
            lev, img, hv, hi, ii, g_h, g_l, xs_h, xs_l, sm,
-           t_yi, t_ye, t_xh, t_xl,
-           packed, halo, corner, local_sem, send_sem, recv_sem):
+           t_yi, t_ye, t_x,
+           packed, halo, corner, relay, local_sem, send_sem, recv_sem):
     row, col = lax.axis_index("row"), lax.axis_index("col")
     n_row, n_col = lax.axis_size("row"), lax.axis_size("col")
     r_up, r_dn = lax.rem(row + 1, n_row), lax.rem(row + n_row - 1, n_row)
@@ -100,7 +106,7 @@
     own = []
     for i, (src, dst) in enumerate((
         (level_hbm, lev.at[R:R + ZL, 0:YL]), (image_hbm, img.at[R:R + ZL, 0:YL]),
-        (y_in, t_yi), (y_ed, t_ye), (x_h, t_xh), (x_l, t_xl),
+        (y_in, t_yi), (y_ed, t_ye), (x_all, t_x),
     )):
         copy = pltpu.make_async_copy(src, dst, local_sem.at[i])
         copy.start()
@@ -130,12 +136,13 @@
                     row0 = YL + 2 + 6 * side
                     block[to + q, row0:row0 + 6, :] = src[side, a, at:at + 6, :]
 
-    sent = {}
-
-    def send(name, axis, target, src, dst, now=True):
+    sent, slots = {}, {}
+
+    def send(name, axis, target, src, dst, now=True, lands=None):
         i = len(sent)
+        slots[name] = i if lands is None else slots[lands]
         copy = pltpu.make_async_remote_copy(
-            src_ref=src, dst_ref=dst, send_sem=send_sem.at[i], recv_sem=recv_sem.at[i],
+            src_ref=src, dst_ref=dst, send_sem=send_sem.at[i], recv_sem=recv_sem.at[slots[name]],
             device_id={axis: target}, device_id_type=MESH,
         )
         if now:
@@ -152,19 +159,60 @@
         for side, target in ((0, r_up), (1, r_dn)):
             send((name, side), "row", target, packed.at[side, :, rows], halo.at[side, :, rows])
 
+    other = row + 1 - 2 * lax.rem(row, 2)
+    outer_row = jnp.logical_or(lax.rem(row, 4) == 0, lax.rem(row, 4) == 3)
+    wraps = (lax.rem(col, 8) == 7, lax.rem(col, 8) == 0)
+    corner_way = [jnp.logical_and(outer_row, w) for w in wraps]
+    helper_way = [jnp.logical_and(jnp.logical_not(outer_row), w) for w in wraps]
+    arrays = ((level_hbm, lev), (image_hbm, img))
+    upper, lower = pl.ds(0, 24), pl.ds(24, 24)
+    z_ways = ((c_up, ZL - 2, R - 2, ZL - R, 0), (c_dn, 0, R + ZL, 2, R + ZL + 2))
+    for way, (target, two, two_to, four, four_to) in enumerate(z_ways):
+        for a, (src, dst) in enumerate(arrays):
+            send(("two", way, a), "col", target, src.at[pl.ds(two, 2)], dst.at[pl.ds(two_to, 2), pl.ds(0, YL)], False)
+            for name, rows in (("upper", upper), ("lower", lower)):
+                send((name, way, a), "col", target, src.at[pl.ds(four, 4), rows], dst.at[pl.ds(four_to, 4), rows], False)
+            send(("first", way, a), "row", other, src.at[pl.ds(four, 4), lower], relay.at[0, a], False,
+                 ("first", 0, a) if way else None)
+        send(("second", way), "col", target, relay.at[0], relay.at[1], False, ("second", 0) if way else None)
+    for way, (_, _, _, _, four_to) in enumerate(z_ways):
+        for a, (_, dst) in enumerate(arrays):
+            send(("third", way, a), "row", other, relay.at[1, a], dst.at[pl.ds(four_to, 4), lower], False,
+                 ("lower", way, a))
+
+    def start(*names):
+        for name in names:
+            sent[name].start()
+
+    def by_way(predicates, action):
+        for way in (0, 1):
+            pl.when(predicates[way])(functools.partial(action, way))
+
     own[0].wait()
     own[1].wait()
     pack(PARTS["low"])
     pack(PARTS["high"])
     pl.semaphore_wait(barrier, 4)
+    by_way(corner_way, lambda way: start(("first", way, 0), ("first", way, 1)))
     send_part("low")
     send_part("high")
     pack(PARTS["middle"])
     send_part("middle")
-    low, high, own_rows = pl.ds(0, R), pl.ds(ZL - R, R), pl.ds(0, YL)
-    for a, (src, dst) in enumerate(((level_hbm, lev), (image_hbm, img))):
-        send(("above", a), "col", c_up, src.at[high], dst.at[pl.ds(0, R), own_rows])
-        send(("below", a), "col", c_dn, src.at[low], dst.at[pl.ds(R + ZL, R), own_rows])
+    start(*[("two", way, a) for way in (0, 1) for a in (0, 1)])
+    direct_way = [jnp.logical_not(p) for p in corner_way]
+    upper_now = [jnp.logical_not(p) for p in helper_way]
+    lower_now = [jnp.logical_not(jnp.logical_or(p, q)) for p, q in zip(corner_way, helper_way)]
+    by_way(upper_now, lambda way: start(("upper", way, 0), ("upper", way, 1)))
+    by_way(lower_now, lambda way: start(("lower", way, 0), ("lower", way, 1)))
+
+    def forward(way):
+        arrived(("first", 0, 0), ("first", 0, 1))
+        start(("second", way), *[(name, way, a) for name in ("upper", "lower") for a in (0, 1)])
+
+    def deliver(way):
+        arrived(("second", 0))
+        start(("third", 1 - way, 0), ("third", 1 - way, 1))
+
     outer = {"corner above": (c_up, PARTS["high"], 0), "corner below": (c_dn, PARTS["low"], 1)}
     for name, (target, part, way) in outer.items():
         send(name, "col", target, halo.at[:, :, pl.ds(part.start, part.size)], corner.at[way], False)
@@ -203,18 +251,29 @@
     def smooth_y(g, table, depth, base):
         planes = pl.ds(g * G, G)
         m = table.shape[0] // 2
-        for k in range(4):
-            high = g_h[k, planes, 0:depth, :].reshape(G * depth, N)
-            low = g_l[k, planes, 0:depth, :].reshape(G * depth, N)
-            y = dot(table[...], high)
-            y = y[0:m] + y[m:2 * m] + dot(table[0:m, :], low)
-            yh = y.astype(BF16)
-            xs_h[k * 128 + base:k * 128 + base + m, :] = yh
-            xs_l[k * 128 + base:k * 128 + base + m, :] = (y - yh.astype(F32)).astype(BF16)
+        high = [g_h[k, planes, 0:depth, :].reshape(G * depth, N) for k in range(4)]
+        low = [g_l[k, planes, 0:depth, :].reshape(G * depth, N) for k in range(4)]
+        for k in range(0, 4, 2):
+            pair = dot(table[...], jnp.concatenate(high[k:k + 2], axis=1))
+            pair = pair[0:m] + pair[m:2 * m] + dot(table[0:m, :], jnp.concatenate(low[k:k + 2], axis=1))
+            for f in (0, 1):
+                y = pair[:, f * N:(f + 1) * N]
+                rows = slice((k + f) * 128 + base, (k + f) * 128 + base + m)
+                for w, start in enumerate(WINDOWS):
+                    part = pltpu.roll(y, -start % N, 1)[:, 0:256]
+                    ph = part.astype(BF16)
+                    xs_h[w, rows, :] = ph
+                    xs_l[w, rows, :] = (part - ph.astype(F32)).astype(BF16)
 
     def smooth_x():
-        a = xs_h[...]
-        sm[...] = dot(a, t_xh[...]) + dot(a, t_xl[...]) + dot(xs_l[...], t_xh[...])
+        for w in (0, 1):
+            a = xs_h[w]
+            part = dot(jnp.concatenate([a, xs_l[w], a], axis=1), t_x[w])
+            if w == 0:
+                sm[:, 0:256] = part
+            else:
+                sm[:, 128:256] = sm[:, 128:256] + part[:, 0:128]
+                sm[:, 256:384] = part[:, 128:256]
 
     def pointwise(p, rows, base, up, down):
         s1, s2, s3, s4 = (sm[base + k * 128:base + k * 128 + 8, :] for k in range(4))
@@ -266,12 +325,8 @@
     near = jnp.where(even, 1, 0)
     far = 1 - near
 
-    def z_halo(side):
-        for way, name in ((0, "above"), (1, "below")):
-            @pl.when(side == way)
-            def _():
-                arrived((name, 0), (name, 1))
-        fields(side * (R + ZL), R, 0, YL, 16)
+    def z_arrived(side, *names):
+        by_way((side == 0, side == 1), lambda way: arrived(*[(name, way, a) for name in names for a in (0, 1)]))
 
     def corner_halo(side):
         for way, name in ((0, "corner above"), (1, "corner below")):
@@ -287,11 +342,18 @@
 
     @pl.loop(0, 4)
     def _(i):
+        @pl.when(i == 1)
+        def _():
+            by_way(helper_way, forward)
+
         @pl.when(i == 2)
         def _():
-            z_halo(near)
+            z_arrived(near, "two", "upper", "lower")
+            fields(near * (R + ZL), R, 0, YL, 16)
 
         inner(jnp.where(i < 2, i + 2, near * 4 + i - 2))
+
+    by_way(helper_way, deliver)
 
     arrived(("low", 0), ("low", 1), ("high", 0), ("high", 1))
     for name in outer:
@@ -309,17 +371,32 @@
 
         edge(jnp.where(i == 0, 1, near * 2))
 
-    z_halo(far)
-
     @pl.loop(0, 2)
     def _(i):
-        inner(far * 4 + i)
+        @pl.when(i == 0)
+        def _():
+            z_arrived(far, "two")
+            fields(far * (R + ZL - 4) + 4, 2, 0, YL, 16)
+
+        @pl.when(i == 1)
+        def _():
+            z_arrived(far, "upper", "lower")
+            fields(far * (R + ZL + 2), 4, 0, YL, 16)
+
+        inner(jnp.where(i == 0, 1 + 3 * far, 5 * far))
 
     corner_halo(far)
     edge(far * 2)
 
-    for copy in sent.values():
-        copy.wait_send()
+    def all_sent(*names):
+        for name in names:
+            sent[name].wait_send()
+
+    held = ("lower", "first", "second", "third")
+    all_sent(*[name for name in sent if name[0] not in held])
+    by_way(direct_way, lambda way: all_sent(("lower", way, 0), ("lower", way, 1)))
+    by_way(corner_way, lambda way: all_sent(("first", way, 0), ("first", way, 1)))
+    by_way(helper_way, lambda way: all_sent(("second", way), ("third", 1 - way, 0), ("third", 1 - way, 1)))
 
 
 def step(level_set, image):
@@ -330,13 +407,13 @@
     return pl.pallas_call(
         kernel,
         out_shape=jax.ShapeDtypeStruct((ZL, YL, N), F32),
-        in_specs=[pl.BlockSpec(memory_space=pltpu.HBM)] * 6,
+        in_specs=[pl.BlockSpec(memory_space=pltpu.HBM)] * 5,
         out_specs=pl.BlockSpec(memory_space=pltpu.VMEM),
-        scratch_shapes=[ext] * 5 + [half, half, pltpu.VMEM((rows, N), BF16), pltpu.VMEM((rows, N), BF16),
+        scratch_shapes=[ext] * 5 + [half, half, pltpu.VMEM((2, rows, 256), BF16), pltpu.VMEM((2, rows, 256), BF16),
                                     pltpu.VMEM((rows, N), F32)]
         + [pltpu.VMEM(c.shape, BF16) for c in consts]
-        + [pltpu.VMEM((2, 2, PACKED, N), F32)] * 2 + [pltpu.VMEM((2, 2, 2, 40, N), F32)]
-        + [pltpu.SemaphoreType.DMA((8,)), pltpu.SemaphoreType.DMA((12,)), pltpu.SemaphoreType.DMA((12,))],
+        + [pltpu.VMEM((2, 2, PACKED, N), F32)] * 2 + [pltpu.VMEM((2, 2, 2, 40, N), F32), pltpu.VMEM((2, 2, 4, 24, N), F32)]
+        + [pltpu.SemaphoreType.DMA((8,)), pltpu.SemaphoreType.DMA((40,)), pltpu.SemaphoreType.DMA((40,))],
         compiler_params=pltpu.CompilerParams(
             collective_id=0, has_side_effects=True, vmem_limit_bytes=48 * 1024 * 1024),
     )(*[pltpu.with_memory_space_constraint(v, pltpu.HBM) for v in (level_set, image, *consts)])

time: 39.3 us -> 34.1 us (0.87)
  Pallas kernels: 38 us -> 32.4 us
    pallas_call x1, Pallas kernels: 38 us -> 32.4 us  [step(): pl.pallas_call(kernel, out_shape=jax.ShapeDtypeStruct((ZL, YL, N), F32),...]
where the time goes in v5:
time: 34.1 us; the launch traced here: 33.7 us
  Pallas kernels  32.4 us (95%)
  local copies, waits for them, and re-layouts  1.21 us (4%)
    pallas_call x1, Pallas kernels, step(): pl.pallas_call(kernel, out_shape=jax.ShapeDtypeStruct((ZL, YL, N), F32),...  32.4 us
    unnamed x1, local copies, waits for them, and re-layouts  1.21 us

profile of v5, /device:TPU:0, one launch (start us, length us, event | category | flops | bytes accessed | tf_op | source)
XLA Modules:
  0.0 33.7 jit_solution(9987959847753410)
XLA Ops:
  0.0 32.4 %shard_map.55 = f32[24,48,384]{2,1,0:T(8,128)S(1)} custom-call(f32[24,48,384]{2,1,0:T(8,128)} %level_hbm.1, f32[24,48,384]{2,1,0:T(8,128)} %image_hbm.1, bf16[256,192]{1,0:T(8,128)(2,1)} %constant.6.clone.y_in, bf16[128,256]{1,0:T(8,128)(2,1)} %constant.7.clone.y_ed, bf16[2,768,256]{2,1,0:T(8,128)(2,1)} %constant.8.clone.x_all), custom_call_target="tpu_custom_call" | custom-call | tf_op jit(solution)/shard_map/pallas_call | solution.py:407
  32.4 1.2 %copy.7 = f32[24,48,384]{2,1,0:T(8,128)} copy(f32[24,48,384]{2,1,0:T(8,128)S(1)} %shard_map.55) | data formatting | bytes 3538944

commit v6 on v5

--- a/solution.py
+++ b/solution.py
@@ -78,16 +78,14 @@
 
 
 def heaviside(level):
-    size = jnp.abs(level)
-    big = size > 1.0
-    t = jnp.where(big, 1.0 / jnp.maximum(size, 1.0), size)
+    big = jnp.abs(level) > 1.0
+    t = jnp.where(big, 1.0 / jnp.where(big, level, 1.0), level)
     u = t * t
     q = jnp.full_like(u, ATAN[-1])
     for coeff in ATAN[-2::-1]:
         q = q * u + coeff
     q = q * t
-    q = jnp.where(big, 0.5 - q, q)
-    return 0.5 + jnp.where(level < 0.0, -q, q)
+    return jnp.where(big, jnp.where(level > 0.0, 1.0, 0.0) - q, 0.5 + q)
 
 
 def kernel(level_hbm, image_hbm, y_in, y_ed, x_all, out_ref,
@@ -112,8 +110,6 @@
         copy.start()
         own.append(copy)
 
-    for block in (lev, img):
-        block[:, YL:YE, :] = jnp.zeros((ZE, YE - YL, N), F32)
     for side in (0, 1):
         for a in (0, 1):
             for part in PARTS.values():
@@ -218,32 +214,42 @@
         send(name, "col", target, halo.at[:, :, pl.ds(part.start, part.size)], corner.at[way], False)
 
     def fields(first, count, start, size, step):
-        @pl.loop(first, first + count)
-        def _(p):
+        @pl.loop(0, count // 2)
+        def _(i):
+            planes = pl.ds(first + 2 * i, 2)
             for s in range(start, start + size, step):
                 rows = slice(s, s + step)
-                h = heaviside(lev[p, rows, :])
-                im = img[p, rows, :]
-                hv[p, rows, :] = h
-                hi[p, rows, :] = h * im
-                ii[p, rows, :] = im * im
+                h = heaviside(lev[planes, rows, :])
+                im = img[planes, rows, :]
+                hv[planes, rows, :] = h
+                hi[planes, rows, :] = h * im
+                ii[planes, rows, :] = im * im
 
     weights = taps()
     ratio = [float(np.float32(weights[R + d] / weights[R])) for d in range(R + 1)]
 
     def smooth_z(g, chunk):
         rows = slice(chunk * 16, chunk * 16 + 16)
+        waiting = []
+
+        def store():
+            for k, o, lanes, high, low in waiting:
+                g_h[k, g * G + o, rows, lanes] = high
+                g_l[k, g * G + o, rows, lanes] = low
+            waiting.clear()
+
         for k, ref in enumerate((hi, hv, img, ii)):
             for lt in range(3):
                 lanes = slice(lt * 128, lt * 128 + 128)
                 f = [ref[g * G + j, rows, lanes] for j in range(G + 2 * R)]
+                store()
                 for o in range(G):
                     total = f[o + R]
                     for d in range(1, R + 1):
                         total = total + ratio[d] * (f[o + R - d] + f[o + R + d])
                     high = total.astype(BF16)
-                    g_h[k, g * G + o, rows, lanes] = high
-                    g_l[k, g * G + o, rows, lanes] = (total - high.astype(F32)).astype(BF16)
+                    waiting.append((k, o, lanes, high, (total - high.astype(F32)).astype(BF16)))
+        store()
 
     def dot(a, b):
         return jnp.dot(a, b, preferred_element_type=F32)
@@ -288,13 +294,16 @@
         force = (x1 - x2) * (2.0 * im * both - (x1 + x2)) / (both * both * spread * (np.pi * (1.0 + level * level)))
         lap = (lev[p + R + 1, rows, :] + lev[p + R - 1, rows, :] + up + down
                + pltpu.roll(level, 1, 1) + pltpu.roll(level, N - 1, 1) - 6.0 * level)
-        out_ref[p, rows, :] = level + DT * (NU * lap + force)
+        return level + DT * (NU * lap + force)
 
     def inner_points(g):
         for o in range(G):
             p = g * G + o
-            for s in range(8, 40, 8):
-                pointwise(p, slice(s, s + 8), o * 32 + s - 8, lev[p + R, s + 1:s + 9, :], lev[p + R, s - 1:s + 7, :])
+            for s in range(8, 40, 16):
+                done = [pointwise(p, slice(t, t + 8), o * 32 + t - 8, lev[p + R, t + 1:t + 9, :], lev[p + R, t - 1:t + 7, :])
+                        for t in (s, s + 8)]
+                for t, value in zip((s, s + 8), done):
+                    out_ref[p, t:t + 8, :] = value
 
     sub = lax.broadcasted_iota(jnp.int32, (8, N), 0)
 
@@ -302,10 +311,12 @@
         for o in range(2 * G):
             p = e * 2 * G + o
             down = jnp.where(sub == 0, pltpu.roll(lev[p + R, YL:YL + 8, :], 1, 0), pltpu.roll(lev[p + R, 0:8, :], 1, 0))
-            pointwise(p, slice(0, 8), o * 16, lev[p + R, 1:9, :], down)
             up = jnp.where(sub == 7, pltpu.roll(lev[p + R, YL + 8:YL + 16, :], 7, 0),
                            pltpu.roll(lev[p + R, 40:48, :], 7, 0))
-            pointwise(p, slice(40, 48), o * 16 + 8, up, lev[p + R, 39:47, :])
+            first = pointwise(p, slice(0, 8), o * 16, lev[p + R, 1:9, :], down)
+            last = pointwise(p, slice(40, 48), o * 16 + 8, up, lev[p + R, 39:47, :])
+            out_ref[p, 0:8, :] = first
+            out_ref[p, 40:48, :] = last
 
     def inner(g):
         for chunk in range(3):
@@ -336,6 +347,8 @@
                 unpack(corner.at[way], 0, R, way * (R + ZL))
         fields(side * (R + ZL), R, YL, 16, 16)
 
+    for block in (lev, img):
+        block[:, YL:YE, :] = jnp.zeros((ZE, YE - YL, N), F32)
     fields(R, ZL, 0, YL, 16)
     for copy in own[2:]:
         copy.wait()

time: 34.1 us -> 33.7 us (0.988); the launches traced: 33.7 us -> 33.6 us
  no operation moved by 1% of the time
where the time goes in v6:
time: 33.7 us; the launch traced here: 33.6 us
  Pallas kernels  32.4 us (96%)
  local copies, waits for them, and re-layouts  1.21 us (4%)
    pallas_call x1, Pallas kernels, step(): pl.pallas_call(kernel, out_shape=jax.ShapeDtypeStruct((ZL, YL, N), F32),...  32.4 us
    unnamed x1, local copies, waits for them, and re-layouts  1.21 us

profile of v6, /device:TPU:0, one launch (start us, length us, event | category | flops | bytes accessed | tf_op | source)
XLA Modules:
  0.0 33.6 jit_solution(12852955382623841126)
XLA Ops:
  0.0 32.4 %shard_map.55 = f32[24,48,384]{2,1,0:T(8,128)S(1)} custom-call(f32[24,48,384]{2,1,0:T(8,128)} %level_hbm.1, f32[24,48,384]{2,1,0:T(8,128)} %image_hbm.1, bf16[256,192]{1,0:T(8,128)(2,1)} %constant.6.clone.y_in, bf16[128,256]{1,0:T(8,128)(2,1)} %constant.7.clone.y_ed, bf16[2,768,256]{2,1,0:T(8,128)(2,1)} %constant.8.clone.x_all), custom_call_target="tpu_custom_call" | custom-call | tf_op jit(solution)/shard_map/pallas_call | solution.py:420
  32.4 1.2 %copy.7 = f32[24,48,384]{2,1,0:T(8,128)} copy(f32[24,48,384]{2,1,0:T(8,128)S(1)} %shard_map.55) | data formatting | bytes 3538944

commit v7 on v6

--- a/solution.py
+++ b/solution.py
@@ -184,10 +184,29 @@
         for way in (0, 1):
             pl.when(predicates[way])(functools.partial(action, way))
 
+    def fields(first, count, start, size, step):
+        @pl.loop(0, count // 2)
+        def _(i):
+            planes = pl.ds(first + 2 * i, 2)
+            for s in range(start, start + size, step):
+                rows = slice(s, s + step)
+                h = heaviside(lev[planes, rows, :])
+                im = img[planes, rows, :]
+                hv[planes, rows, :] = h
+                hi[planes, rows, :] = h * im
+                ii[planes, rows, :] = im * im
+
     own[0].wait()
     own[1].wait()
     pack(PARTS["low"])
     pack(PARTS["high"])
+
+    early = jnp.logical_or(lax.rem(row, 4) == 0, col == 0)
+
+    @pl.when(early)
+    def _():
+        fields(R, ZL, 0, YL, 16)
+
     pl.semaphore_wait(barrier, 4)
     by_way(corner_way, lambda way: start(("first", way, 0), ("first", way, 1)))
     send_part("low")
@@ -212,18 +231,6 @@
     outer = {"corner above": (c_up, PARTS["high"], 0), "corner below": (c_dn, PARTS["low"], 1)}
     for name, (target, part, way) in outer.items():
         send(name, "col", target, halo.at[:, :, pl.ds(part.start, part.size)], corner.at[way], False)
-
-    def fields(first, count, start, size, step):
-        @pl.loop(0, count // 2)
-        def _(i):
-            planes = pl.ds(first + 2 * i, 2)
-            for s in range(start, start + size, step):
-                rows = slice(s, s + step)
-                h = heaviside(lev[planes, rows, :])
-                im = img[planes, rows, :]
-                hv[planes, rows, :] = h
-                hi[planes, rows, :] = h * im
-                ii[planes, rows, :] = im * im
 
     weights = taps()
     ratio = [float(np.float32(weights[R + d] / weights[R])) for d in range(R + 1)]
@@ -349,7 +356,10 @@
 
     for block in (lev, img):
         block[:, YL:YE, :] = jnp.zeros((ZE, YE - YL, N), F32)
-    fields(R, ZL, 0, YL, 16)
+    @pl.when(jnp.logical_not(early))
+    def _():
+        fields(R, ZL, 0, YL, 16)
+
     for copy in own[2:]:
         copy.wait()
 

time: 33.7 us -> 33.7 us (level)
  no operation moved by 1% of the time
where the time goes in v7:
time: 33.7 us; the launch traced here: 33.6 us
  Pallas kernels  32.4 us (96%)
  local copies, waits for them, and re-layouts  1.21 us (4%)
    pallas_call x1, Pallas kernels, step(): pl.pallas_call(kernel, out_shape=jax.ShapeDtypeStruct((ZL, YL, N), F32),...  32.4 us
    unnamed x1, local copies, waits for them, and re-layouts  1.21 us

profile of v7, /device:TPU:0, one launch (start us, length us, event | category | flops | bytes accessed | tf_op | source)
XLA Modules:
  0.0 33.6 jit_solution(2078186127712379527)
XLA Ops:
  0.0 32.4 %shard_map.55 = f32[24,48,384]{2,1,0:T(8,128)S(1)} custom-call(f32[24,48,384]{2,1,0:T(8,128)} %level_hbm.1, f32[24,48,384]{2,1,0:T(8,128)} %image_hbm.1, bf16[256,192]{1,0:T(8,128)(2,1)} %constant.6.clone.y_in, bf16[128,256]{1,0:T(8,128)(2,1)} %constant.7.clone.y_ed, bf16[2,768,256]{2,1,0:T(8,128)(2,1)} %constant.8.clone.x_all), custom_call_target="tpu_custom_call" | custom-call | tf_op jit(solution)/shard_map/pallas_call | solution.py:430
  32.4 1.2 %copy.7 = f32[24,48,384]{2,1,0:T(8,128)} copy(f32[24,48,384]{2,1,0:T(8,128)S(1)} %shard_map.55) | data formatting | bytes 3538944
